TPU v7x, 128 devices: a whole 4x4x4 slice. The times are simulated.
128 devices in a mesh: seq: 32 (over z, y, core), head: 4 (over x).
Axes of the slice: x: 4, y: 4, z: 4, core: 2. Of those that a mesh axis runs over, the one named last changes fastest.
Arguments:
- queries: bfloat16 [32768, 4096], P('seq', 'head'), may hold values from -6 to 6
- keys: bfloat16 [32768, 4096], P('seq', 'head'), may hold values from -6 to 6
- values: bfloat16 [32768, 4096], P('seq', 'head'), may hold values from -6 to 6
- cluster_ids: int32 [4, 32768], P('head', 'seq'), may hold values from 0 to 1023, as said below
- slots: int32 [4, 32768], P('head', 'seq'), may hold values from 0 to 2, as said below
- centroid_sums: float32 [4, 1024, 1024], P('head', 'seq'), may hold values from -48 to 48
- centroid_counts: float32 [4, 1024], P('head', 'seq'), may hold values from 8 to 64
- out_weight: bfloat16 [4096, 4096], P('head'), may hold values from -0.09375 to 0.09375
Outputs:
- mixed: bfloat16 [32768, 4096], P(('seq', 'head'))
- centroids: float32 [4, 1024, 1024], P('head', 'seq')
Inputs may be any that keep to these rules, and one draw needn't show every extreme that they name: `cluster_ids`: blocks are the aligned runs of 1024 tokens of one head group. In every block no cluster holds more than 3 tokens, and some cluster holds exactly 3; the clusters k * 32 to (k + 1) * 32 - 1 together hold at most 48 tokens of a block, and exactly 48 for some k in every block. Within one block the tokens of one cluster have slots 0, 1, 2, ... in the order of their positions.
All inputs are finite; a program needn't handle non-finite values.
Results may differ from a plain program's by a relative error of at most 0.015.
Values may be sent and summed in bfloat16 or wider, within the bound.
A program may use at most 192 MiB of HBM per device.

v0:
```python
import jax
import jax.numpy as jnp
from jax import lax
from jax.sharding import PartitionSpec as P

HD = 128
SLOTS = 3


def attend_clusters(cluster_rows, present):
    clusters_here, slot_count, packed_width = cluster_rows.shape
    row_width = packed_width // 3
    head_count = row_width // HD
    query_part = cluster_rows[:, :, :row_width].reshape(clusters_here, slot_count, head_count, HD)
    key_part = cluster_rows[:, :, row_width : 2 * row_width].reshape(
        clusters_here, slot_count, head_count, HD
    )
    value_part = cluster_rows[:, :, 2 * row_width :].reshape(
        clusters_here, slot_count, head_count, HD
    )
    scores = jnp.einsum(
        "crhd,cshd->chrs", query_part, key_part, preferred_element_type=jnp.float32
    ) * HD ** (-0.5)
    slot_index = jnp.arange(slot_count, dtype=jnp.int32)
    allowed = (present[:, None, None, :] > 0) & (
        slot_index[None, None, None, :] <= slot_index[None, None, :, None]
    )
    scores = jnp.where(allowed, scores, -1e30)
    row_max = jnp.max(scores, axis=-1, keepdims=True)
    shifted = jnp.exp(scores - row_max)
    weights = (shifted / jnp.sum(shifted, axis=-1, keepdims=True)).astype(jnp.bfloat16)
    attended = jnp.einsum(
        "chrs,cshd->crhd", weights, value_part, preferred_element_type=jnp.float32
    )
    return attended.astype(jnp.bfloat16).reshape(clusters_here, slot_count, row_width)


def shards(queries, keys, values, cluster_ids, slots, centroid_sums, centroid_counts, out_weight):
    owners = lax.axis_size("seq")
    row_width = queries.shape[1]
    per_owner = centroid_sums.shape[1]
    cluster_of = cluster_ids[0]
    slot_of = slots[0]
    packed = jnp.concatenate([queries, keys, values], axis=1)
    target = cluster_of * SLOTS + slot_of
    outgoing = (
        jnp.zeros((owners * per_owner * SLOTS, 3 * row_width), jnp.bfloat16).at[target].set(packed)
    )
    filled = jnp.zeros((owners * per_owner * SLOTS,), jnp.bfloat16).at[target].set(1.0)
    outgoing = outgoing.reshape(owners, per_owner, SLOTS, 3 * row_width)
    filled = filled.reshape(owners, per_owner, SLOTS)
    cluster_rows, present = (
        lax.all_to_all(outgoing, "seq", split_axis=0, concat_axis=2, tiled=True),
        lax.all_to_all(filled, "seq", split_axis=0, concat_axis=2, tiled=True),
    )
    cluster_rows = cluster_rows[0]
    present = present[0]
    attended = attend_clusters(cluster_rows, present)
    returned = lax.all_to_all(attended[None], "seq", split_axis=2, concat_axis=0, tiled=True)
    own_rows = returned.reshape(owners * per_owner * SLOTS, row_width)[target]
    belongs_all = (
        cluster_of[:, None] == jnp.arange(per_owner * owners, dtype=jnp.int32)[None, :]
    ).astype(jnp.bfloat16)
    part_sums = lax.dot_general(
        belongs_all, keys, (((0,), (0,)), ((), ())), preferred_element_type=jnp.float32
    )
    part_counts = jnp.sum(belongs_all, axis=0, dtype=jnp.float32)
    batch_sums, batch_counts = (
        lax.psum_scatter(
            part_sums.astype(jnp.bfloat16), "seq", scatter_dimension=0, tiled=True
        ).astype(jnp.float32),
        lax.psum_scatter(
            part_counts.astype(jnp.bfloat16), "seq", scatter_dimension=0, tiled=True
        ).astype(jnp.float32),
    )
    fresh_sums = 0.6 * centroid_sums[0] + 0.4 * batch_sums
    fresh_counts = 0.6 * centroid_counts[0] + 0.4 * batch_counts
    centroids = (fresh_sums / fresh_counts[:, None])[None]
    mixed = lax.psum_scatter(
        jnp.dot(own_rows, out_weight, preferred_element_type=jnp.float32).astype(jnp.bfloat16),
        "head",
        scatter_dimension=0,
        tiled=True,
    )
    return (mixed, centroids)


def solution(mesh):
    return jax.shard_map(
        shards,
        mesh=mesh,
        in_specs=(
            P("seq", "head"),
            P("seq", "head"),
            P("seq", "head"),
            P("head", "seq"),
            P("head", "seq"),
            P("head", "seq", None),
            P("head", "seq"),
            P("head", None),
        ),
        out_specs=(P(("seq", "head"), None), P("head", "seq", None)),
        check_vma=False,
    )
```

profile of v0, /device:TPU:1, one launch (start us, length us, event | category | flops | bytes accessed | tf_op | source)
XLA Modules:
  0.0 671.4 jit_solution(9050171877807597479)
XLA Ops:
  7.2 0.7 compare_select_fusion
  7.9 7.6 %scatter_custom_fusion.1 = bf16[3072]{0:T(1024)(128)(2,1)S(1)} fusion(s32[1024]{0:T(1024)S(1)} %bitcast.66, bf16[1024]{0:T(1024)(128)(2,1)S(1)} %broadcast.70, bf16[]{:T(256)} %constant.11.clone.1), kind=kCustom, calls=%fused_computation.35 | custom fusion | bytes 6146 | tf_op jit(solution)/shard_map/scatter | solution.py:49
  15.9 0.9 copy.39
  16.8 9.9 %all-to-all-start.1 = ((bf16[32,32,3]{1,2,0:T(4,128)(2,1)}), bf16[32,32,3]{1,2,0:T(4,128)(2,1)S(1)}, u32[]{:S(2)}, u32[]{:S(2)}) async-start(bf16[32,32,3]{1,2,0:T(4,128)(2,1)} %copy.39), calls=%async_computation.1 | async-start | bytes 65536 | tf_op jit(solution)/shard_map/all_to_all | solution.py:54
  26.7 6.4 pad_maximum_fusion
  33.1 20.7 %scatter_custom_fusion = bf16[3072,3072]{1,0:T(8,128)(2,1)} fusion(s32[1024]{0:T(1024)S(1)} %bitcast.67, bf16[1024,3072]{1,0:T(8,128)(2,1)} %pad_maximum_fusion, bf16[]{:T(256)} %constant.11.clone.1), kind=kCustom, calls=%fused_computation.8 | custom fusion | bytes 18874880 | tf_op jit(solution)/shard_map/scatter | solution.py:47
  53.7 43.1 %reshape.97 = bf16[32,32,3,3072]{3,2,1,0:T(4,128)(2,1)} reshape(bf16[3072,3072]{1,0:T(8,128)(2,1)} %scatter_custom_fusion) | data formatting | bytes 37748736 | tf_op jit(solution)/shard_map/reshape | solution.py:50
  96.9 21.4 %copy.37 = bf16[32,32,3,3072]{3,1,2,0:T(8,128)(2,1)} copy(bf16[32,32,3,3072]{3,2,1,0:T(4,128)(2,1)} %reshape.97) | data formatting | bytes 37748736 | tf_op jit(solution)/shard_map/reshape | solution.py:50
  118.2 7.4 %all-to-all-start = ((bf16[32,32,3,3072]{3,1,2,0:T(8,128)(2,1)}), bf16[32,32,3,3072]{3,1,2,0:T(8,128)(2,1)}, u32[]{:S(2)}, u32[]{:S(2)}) async-start(bf16[32,32,3,3072]{3,1,2,0:T(8,128)(2,1)} %copy.37), calls=%async_computation | async-start | bytes 37748736 | tf_op jit(solution)/shard_map/all_to_all | solution.py:53
  125.8 0.6 broadcast_and_fusion
  126.4 226.5 %all-to-all-done = bf16[32,32,3,3072]{3,1,2,0:T(8,128)(2,1)} async-done(((bf16[32,32,3,3072]{3,1,2,0:T(8,128)(2,1)}), bf16[32,32,3,3072]{3,1,2,0:T(8,128)(2,1)}, u32[]{:S(2)}, u32[]{:S(2)}) %all-to-all-start) | async-done | bytes 18874400 | tf_op jit(solution)/shard_map/all_to_all | solution.py:53
  353.0 7.9 %fusion.28 = (bf16[32,96,1024]{2,0,1:T(8,128)(2,1)S(1)}, bf16[32,96,1024]{2,0,1:T(8,128)(2,1)S(1)}, bf16[32,96,1024]{2,0,1:T(8,128)(2,1)S(1)}) fusion(bf16[32,96,3072]{2,0,1:T(8,128)(2,1)} %bitcast.4), kind=kLoop, calls=%fused_computation.43 | loop fusion | bytes 37748736 | tf_op jit(solution)/shard_map/slice | solution.py:18
  360.9 4.2 copy.60
  365.1 4.2 copy.61
  369.3 4.3 copy.59
  373.6 17.0 %fusion.5 = f32[32,8,96,96]{2,3,1,0:T(8,128)} fusion(bf16[32,96,8,128]{3,2,0,1:T(8,128)(2,1)} %bitcast.62, bf16[32,96,8,128]{3,2,0,1:T(8,128)(2,1)} %bitcast.61), kind=kOutput, calls=%fused_computation.13 | convolution fusion | flops 603979776 | bytes 22020096 | tf_op jit(solution)/shard_map/crhd,cshd->chrs/dot_general | solution.py:21
  390.6 15.1 %fusion.29 = (f32[32,8,96]{2,1,0:T(8,128)S(1)}, f32[32,8,96,96]{2,3,1,0:T(8,128)}) fusion(f32[32,8,96,96]{2,3,1,0:T(8,128)} %fusion.5, pred[32,96,96]{1,2,0:T(8,128)(4,1)S(1)} %broadcast_and_fusion), kind=kOutput, calls=%fused_computation.44 | output fusion | flops 14155871 | bytes 19267584 | tf_op jit(solution)/shard_map/sub | solution.py:30
  405.8 11.5 %convert_bitcast_fusion = bf16[32,96,8,128]{3,1,2,0:T(8,128)(2,1)} fusion(f32[32,8,96,96]{2,3,1,0:T(8,128)} %get-tuple-element.6, f32[32,8,96]{2,1,0:T(8,128)S(1)} %get-tuple-element.5, bf16[32,96,8,128]{3,2,0,1:T(8,128)(2,1)S(1)} %bitcast.65), kind=kOutput, calls=%fused_computation.17 | convolution fusion | flops 611844096 | bytes 22118400 | tf_op jit(solution)/shard_map/chrs,cshd->crhd/dot_general | solution.py:32
  417.2 7.9 %copy.57 = bf16[32,96,8,128]{3,2,0,1:T(8,128)(2,1)} copy(bf16[32,96,8,128]{3,1,2,0:T(8,128)(2,1)} %convert_bitcast_fusion) | data formatting | bytes 12582912 | tf_op jit(solution)/shard_map/broadcast_in_dim;reshape | solution.py:59
  425.1 10.3 %reshape.130 = bf16[1,32,96,1024]{3,1,0,2:T(8,128)(2,1)} reshape(bf16[32,96,8,128]{3,2,0,1:T(8,128)(2,1)} %copy.57) | data formatting | bytes 12582912 | tf_op jit(solution)/shard_map/broadcast_in_dim;reshape | solution.py:59
  435.4 18.2 %all-to-all-start.2 = ((bf16[1,32,96,1024]{3,1,0,2:T(8,128)(2,1)}), bf16[1,32,96,1024]{3,1,0,2:T(8,128)(2,1)}, u32[]{:S(2)}, u32[]{:S(2)}) async-start(bf16[1,32,96,1024]{3,1,0,2:T(8,128)(2,1)} %reshape.130), calls=%async_computation.2 | async-start | bytes 12582912 | tf_op jit(solution)/shard_map/all_to_all | solution.py:59
  453.7 3.8 fusion.19
  457.8 71.9 %all-to-all-done.2 = bf16[1,32,96,1024]{3,1,0,2:T(8,128)(2,1)} async-done(((bf16[1,32,96,1024]{3,1,0,2:T(8,128)(2,1)}), bf16[1,32,96,1024]{3,1,0,2:T(8,128)(2,1)}, u32[]{:S(2)}, u32[]{:S(2)}) %all-to-all-start.2) | async-done | bytes 6291488 | tf_op jit(solution)/shard_map/all_to_all | solution.py:59
  529.7 12.0 %copy.49 = bf16[32,1,32,3,1024]{4,3,2,0,1:T(4,128)(2,1)} copy(bf16[32,1,32,3,1024]{4,2,3,0,1:T(8,128)(2,1)} %bitcast.11) | data formatting | bytes 12582912 | tf_op jit(solution)/shard_map/all_to_all | solution.py:59
  541.7 16.3 %reshape.102 = bf16[3072,1024]{1,0:T(8,128)(2,1)} reshape(bf16[32,1,32,3,1024]{4,3,2,0,1:T(4,128)(2,1)} %copy.49) | data formatting | bytes 12582912 | tf_op jit(solution)/shard_map/reshape | solution.py:60
  558.1 8.6 %gather_fusion = bf16[1024,1024]{1,0:T(8,128)(2,1)S(1)} fusion(bf16[3072,1024]{1,0:T(8,128)(2,1)} %reshape.102, s32[1024]{0:T(1024)S(1)} %broadcast_clamp_fusion), kind=kCustom, calls=%fused_computation | custom fusion | bytes 4198400 | tf_op jit(solution)/shard_map/gather | solution.py:60
  566.6 14.2 %convolution_convert_fusion = bf16[1024,4096]{1,0:T(8,128)(2,1)} fusion(bf16[1024,1024]{1,0:T(8,128)(2,1)S(1)} %gather_fusion, bf16[1024,4096]{1,0:T(8,128)(2,1)} %param.15), kind=kOutput, calls=%fused_computation.10 | convolution fusion | flops 8594128896 | bytes 18874368 | tf_op jit(solution)/shard_map/dot_general | solution.py:80
  580.9 0.6 copy-done.4
  581.5 0.6 dynamic-slice
  583.2 66.9 %all-reduce = bf16[1024]{0:T(1024)(128)(2,1)S(1)} all-reduce(bf16[1024]{0:T(1024)(128)(2,1)S(1)} %fusion.17), channel_id=4, replica_groups=mesh['seq'=32,'head'=4] {'seq'}, use_global_device_ids=true, to_apply=%region_7.8.clone | all-reduce | flops 1024 | bytes 4096
  650.2 1.6 fusion.21
  651.8 12.5 %reduce-scatter.3.cloned.1.call-done = bf16[256,4096]{1,0:T(8,128)(2,1)} async-done(((bf16[1024,4096]{1,0:T(8,128)(2,1)}), bf16[256,4096]{1,0:T(8,128)(2,1)}) %reduce-scatter.3.cloned.1.call-update) | async-done | bytes 2097168 | tf_op jit(solution)/shard_map/reduce_scatter | solution.py:79
  (29 shorter events, 1.5 us)
Async XLA Ops:
  16.8 101.4 %all-to-all-start.1 = ((bf16[32,32,3]{1,2,0:T(4,128)(2,1)}), bf16[32,32,3]{1,2,0:T(4,128)(2,1)S(1)}, u32[]{:S(2)}, u32[]{:S(2)}) async-start(bf16[32,32,3]{1,2,0:T(4,128)(2,1)} %copy.39), calls=%async_computation.1 | async-start | bytes 65536 | tf_op jit(solution)/shard_map/all_to_all | solution.py:54
  118.2 234.7 %all-to-all-start = ((bf16[32,32,3,3072]{3,1,2,0:T(8,128)(2,1)}), bf16[32,32,3,3072]{3,1,2,0:T(8,128)(2,1)}, u32[]{:S(2)}, u32[]{:S(2)}) async-start(bf16[32,32,3,3072]{3,1,2,0:T(8,128)(2,1)} %copy.37), calls=%async_computation | async-start | bytes 37748736 | tf_op jit(solution)/shard_map/all_to_all | solution.py:53
  373.6 32.1 %slice-start = ((s8[6291456]{0:T(1024)(128)(4,1)}), s8[2097152]{0:T(1024)(128)(4,1)S(1)}, s32[]{:S(2)}) async-start(s8[6291456]{0:T(1024)(128)(4,1)} %bitcast.63), calls=%async_computation.7 | async-start | bytes 4194304
  390.6 15.1 %slice-start.1 = ((s8[6291456]{0:T(1024)(128)(4,1)}), s8[4194304]{0:T(1024)(128)(4,1)S(1)}, s32[]{:S(2)}) async-start(s8[6291456]{0:T(1024)(128)(4,1)} %bitcast.63), calls=%async_computation.8 | async-start | bytes 8388608
  435.4 18.3 %copy-start = (bf16[1024,1024]{1,0:T(8,128)(2,1)S(1)}, bf16[1024,1024]{1,0:T(8,128)(2,1)}, u32[]{:S(2)}) copy-start(bf16[1024,1024]{1,0:T(8,128)(2,1)} %param.9) | copy-start | bytes 6291460
  435.4 18.3 %copy-start.2 = (s32[1,1024]{1,0:T(1,128)S(1)}, s32[1,1024]{1,0:T(1,128)}, u32[]{:S(2)}) copy-start(s32[1,1024]{1,0:T(1,128)} %param.11) | copy-start | bytes 12292
  435.4 94.3 %all-to-all-start.2 = ((bf16[1,32,96,1024]{3,1,0,2:T(8,128)(2,1)}), bf16[1,32,96,1024]{3,1,0,2:T(8,128)(2,1)}, u32[]{:S(2)}, u32[]{:S(2)}) async-start(bf16[1,32,96,1024]{3,1,0,2:T(8,128)(2,1)} %reshape.130), calls=%async_computation.2 | async-start | bytes 12582912 | tf_op jit(solution)/shard_map/all_to_all | solution.py:59
  453.6 196.6 %reduce-scatter.5.cloned.1.call-start = ((), (), s32[]{:S(2)}) async-start(), calls=%async_computation.6 | async-start | bytes 2162688 | tf_op jit(solution)/shard_map/reduce_scatter | solution.py:69
  457.5 206.8 %reduce-scatter.3.cloned.1.call-start = ((), (), s32[]{:S(2)}) async-start(), calls=%async_computation.5 | async-start | bytes 10485760 | tf_op jit(solution)/shard_map/reduce_scatter | solution.py:79
  580.8 0.7 copy-start.4
  580.8 69.3 %copy-start.3 = (f32[1,32]{1,0:T(1,128)S(1)}, f32[1,32]{1,0:T(1,128)}, u32[]{:S(2)}) copy-start(f32[1,32]{1,0:T(1,128)} %param.14) | copy-start | bytes 388
  580.8 69.4 %copy-start.1 = (f32[1,32,1024]{2,1,0:T(8,128)S(1)}, f32[1,32,1024]{2,1,0:T(8,128)}, u32[]{:S(2)}) copy-start(f32[1,32,1024]{2,1,0:T(8,128)} %param.13) | copy-start | bytes 393220
Sparse Core Ops, SparseCore 0:
  458.0 95.8 reduce-scatter.4
  581.0 83.2 reduce-scatter.2
where the time goes:
time: 678 us; the launch traced here: 671 us
  waiting for transfers between devices  311 us (46%)
  local copies, waits for them, and re-layouts  171 us (25%)
  blocking collectives  66.9 us (10%)
  matrix products  46.5 us (7%)
  starting transfers between devices  35.8 us (5%)
  other arithmetic  25 us (4%)
  between operations  15.1 us (2%)
    all_to_all x1, waiting for transfers between devices, shards(): lax.all_to_all(outgoing, 'seq', split_axis=0, concat_axis=2, tiled=True)  227 us
    all_to_all x1, waiting for transfers between devices, shards(): lax.all_to_all(attended[None], 'seq', split_axis=2, concat_axis=0, tiled=...  71.9 us
    unnamed x1, blocking collectives  66.9 us
    reshape x2, local copies, waits for them, and re-layouts, shards(): outgoing = outgoing.reshape(owners, per_owner, SLOTS, 3 * row_width)  64.5 us
    scatter x1, local copies, waits for them, and re-layouts, shards(): jnp.zeros((owners * per_owner * SLOTS, 3 * row_width), jnp.bfloat16)  20.7 us
    all_to_all x1, starting transfers between devices, shards(): lax.all_to_all(attended[None], 'seq', split_axis=2, concat_axis=0, tiled=...  18.2 us
    another operation x2, local copies, waits for them, and re-layouts, shards(): attended[None]  18.2 us
    dot_general x1, matrix products, attend_clusters(): jnp.einsum('crhd,cshd->chrs', query_part, key_part, preferred_element_typ...  17 us
  transfers between devices with their start and end apart: 5, of which 3 were waited for; matrix products, arithmetic and copies ran while one was open for 22% of the time, Pallas kernels for 0%

commit v1 on v0

v1 whole, which is shorter than its diff:
```python
import jax
import jax.numpy as jnp
from jax import lax
from jax.experimental import pallas as pl
from jax.experimental.pallas import tpu as pltpu
from jax.sharding import PartitionSpec as P

HD = 128
SLOTS = 3
SEGMENT = 48
TILE = 128
PACK_ROWS = 192
OUT_COLS = 512
NEG = -1e30


def pack_kernel(position_ref, queries_ref, keys_ref, values_ref, packed_ref):
    width = queries_ref.shape[1]
    rows, tokens = packed_ref.shape[0], queries_ref.shape[0]
    first = pl.program_id(0) * rows
    row_of = first + lax.broadcasted_iota(jnp.int32, (rows, tokens), 0)
    pick = (row_of == position_ref[...]).astype(jnp.bfloat16)
    for index, ref in enumerate((queries_ref, keys_ref, values_ref)):
        packed_ref[:, index * width : (index + 1) * width] = jnp.dot(
            pick, ref[...], preferred_element_type=jnp.float32
        ).astype(jnp.bfloat16)


def pack(position, queries, keys, values, rows):
    tokens, width = queries.shape
    whole = pl.BlockSpec((tokens, width), lambda i: (0, 0))
    return pl.pallas_call(
        pack_kernel,
        grid=(rows // PACK_ROWS,),
        in_specs=[pl.BlockSpec((1, tokens), lambda i: (0, 0)), whole, whole, whole],
        out_specs=pl.BlockSpec((PACK_ROWS, 3 * width), lambda i: (i, 0)),
        out_shape=jax.ShapeDtypeStruct((rows, 3 * width), jnp.bfloat16),
    )(position.reshape(1, tokens), queries, keys, values)


def attend_kernel(
    row_target_ref,
    column_target_ref,
    cluster_ref,
    first_ref,
    rows_ref,
    sums_ref,
    counts_ref,
    returned_ref,
    centroids_ref,
    ordered_ref,
    attended_ref,
):
    rows, packed_width = rows_ref.shape
    width = packed_width // 3
    clusters = sums_ref.shape[0]
    tiles = rows // TILE

    belongs = lax.broadcasted_iota(jnp.int32, (clusters, rows), 0) == cluster_ref[...]
    batch_sums = jnp.dot(
        belongs.astype(jnp.bfloat16),
        rows_ref[:, width : 2 * width],
        preferred_element_type=jnp.float32,
    )
    batch_counts = jnp.sum(belongs.astype(jnp.float32), axis=1, keepdims=True)
    centroids_ref[...] = (0.6 * sums_ref[...] + 0.4 * batch_sums) / (
        0.6 * counts_ref[...] + 0.4 * batch_counts
    )

    ordered_ref[0:TILE, :] = jnp.zeros((TILE, packed_width), jnp.bfloat16)

    def order(step, carry):
        start = step * (2 * TILE)
        place = start + lax.broadcasted_iota(jnp.int32, (2 * TILE, rows), 0)
        pick = (place == row_target_ref[...]).astype(jnp.bfloat16)
        for part in range(3):
            ordered_ref[pl.ds(start + TILE, 2 * TILE), part * width : (part + 1) * width] = (
                jnp.dot(
                    pick,
                    rows_ref[:, part * width : (part + 1) * width],
                    preferred_element_type=jnp.float32,
                ).astype(jnp.bfloat16)
            )
        return carry

    lax.fori_loop(0, tiles // 2, order, 0)

    def attend(step, carry):
        start = step * TILE
        place = start + lax.broadcasted_iota(jnp.int32, (TILE, first_ref.shape[1]), 0)
        first = first_ref[...]
        low = jnp.max(jnp.where(first <= place, first, 0), axis=1, keepdims=True)
        query_place = start + lax.broadcasted_iota(jnp.int32, (TILE, 2 * TILE), 0)
        key_place = start - TILE + lax.broadcasted_iota(jnp.int32, (TILE, 2 * TILE), 1)
        seen = (key_place <= query_place) & (key_place >= low)
        for head in range(width // HD):
            column = head * HD
            query = ordered_ref[pl.ds(start + TILE, TILE), column : column + HD]
            key = ordered_ref[pl.ds(start, 2 * TILE), width + column : width + column + HD]
            value = ordered_ref[
                pl.ds(start, 2 * TILE), 2 * width + column : 2 * width + column + HD
            ]
            scores = lax.dot_general(
                query, key, (((1,), (1,)), ((), ())), preferred_element_type=jnp.float32
            ) * (HD**-0.5)
            scores = jnp.where(seen, scores, NEG)
            shifted = jnp.exp(scores - jnp.max(scores, axis=1, keepdims=True))
            weights = shifted / jnp.sum(shifted, axis=1, keepdims=True)
            attended_ref[pl.ds(start, TILE), column : column + HD] = jnp.dot(
                weights.astype(jnp.bfloat16), value, preferred_element_type=jnp.float32
            ).astype(jnp.bfloat16)
        return carry

    lax.fori_loop(0, tiles, attend, 0)

    def restore(step, carry):
        start = step * (2 * TILE)
        target = column_target_ref[pl.ds(start, 2 * TILE), :]
        pick = (lax.broadcasted_iota(jnp.int32, (2 * TILE, rows), 1) == target).astype(jnp.bfloat16)
        returned_ref[pl.ds(start, 2 * TILE), :] = jnp.dot(
            pick, attended_ref[...], preferred_element_type=jnp.float32
        ).astype(jnp.bfloat16)
        return carry

    lax.fori_loop(0, tiles // 2, restore, 0)


def attend_clusters(target, cluster, first, rows, sums, counts):
    total, packed_width = rows.shape
    width = packed_width // 3
    clusters = sums.shape[0]
    vmem = pl.BlockSpec(memory_space=pltpu.VMEM)
    return pl.pallas_call(
        attend_kernel,
        in_specs=[vmem] * 7,
        out_specs=[vmem] * 2,
        out_shape=[
            jax.ShapeDtypeStruct((total, width), jnp.bfloat16),
            jax.ShapeDtypeStruct((clusters, width), jnp.float32),
        ],
        scratch_shapes=[
            pltpu.VMEM((total + TILE, packed_width), jnp.bfloat16),
            pltpu.VMEM((total, width), jnp.bfloat16),
        ],
        compiler_params=pltpu.CompilerParams(vmem_limit_bytes=60 << 20),
    )(
        target.reshape(1, total),
        target.reshape(total, 1),
        cluster.reshape(1, total),
        first,
        rows,
        sums,
        counts,
    )


def project_kernel(position_ref, rows_ref, weight_ref, out_ref, own_ref):
    tokens, total = own_ref.shape[0], rows_ref.shape[0]

    @pl.when(pl.program_id(0) == 0)
    def _():
        pick = (lax.broadcasted_iota(jnp.int32, (tokens, total), 1) == position_ref[...]).astype(
            jnp.bfloat16
        )
        own_ref[...] = jnp.dot(pick, rows_ref[...], preferred_element_type=jnp.float32).astype(
            jnp.bfloat16
        )

    out_ref[...] = jnp.dot(
        own_ref[...], weight_ref[...], preferred_element_type=jnp.float32
    ).astype(jnp.bfloat16)


def project(position, rows, weight):
    tokens = position.shape[0]
    total, width = rows.shape
    columns = weight.shape[1]
    return pl.pallas_call(
        project_kernel,
        grid=(columns // OUT_COLS,),
        in_specs=[
            pl.BlockSpec((tokens, 1), lambda i: (0, 0)),
            pl.BlockSpec((total, width), lambda i: (0, 0)),
            pl.BlockSpec((width, OUT_COLS), lambda i: (0, i)),
        ],
        out_specs=pl.BlockSpec((tokens, OUT_COLS), lambda i: (0, i)),
        out_shape=jax.ShapeDtypeStruct((tokens, columns), jnp.bfloat16),
        scratch_shapes=[pltpu.VMEM((tokens, width), jnp.bfloat16)],
    )(position.reshape(tokens, 1), rows, weight)


def block_positions(cluster_of, owners, per_owner):
    tokens = cluster_of.shape[0]
    owner_of = cluster_of // per_owner
    belongs = (jnp.arange(owners, dtype=jnp.int32)[:, None] == owner_of[None, :]).astype(
        jnp.bfloat16
    )
    token = jnp.arange(tokens, dtype=jnp.int32)
    earlier = (token[:, None] < token[None, :]).astype(jnp.bfloat16)
    before = jnp.dot(belongs, earlier, preferred_element_type=jnp.float32)
    rank = jnp.sum(before * belongs.astype(jnp.float32), axis=0)
    return owner_of * SEGMENT + rank.astype(jnp.int32)


def sorted_targets(codes, per_owner):
    owners = codes.shape[0]
    cluster = jnp.where(codes < 0, -1, codes // SLOTS)
    slot = codes % SLOTS
    here = jnp.arange(per_owner, dtype=jnp.int32)
    one_hot = (cluster[:, :, None] == here[None, None, :]).astype(jnp.int32)
    count = jnp.sum(one_hot, axis=1)
    source = jnp.arange(owners, dtype=jnp.int32)
    before = jnp.sum(
        jnp.where((source[None, :] < source[:, None])[:, :, None], count[None, :, :], 0), axis=1
    )
    total = jnp.sum(count, axis=0)
    first = jnp.sum(jnp.where(here[None, :] < here[:, None], total[None, :], 0), axis=1)
    base = first[None, :] + before
    target = jnp.sum(one_hot * base[:, None, :], axis=2) + slot
    return jnp.where(codes < 0, -1, target), cluster, first


def shards(queries, keys, values, cluster_ids, slots, centroid_sums, centroid_counts, out_weight):
    owners = lax.axis_size("seq")
    row_width = queries.shape[1]
    per_owner = centroid_sums.shape[1]
    total = owners * SEGMENT
    cluster_of = cluster_ids[0]
    slot_of = slots[0]
    position = block_positions(cluster_of, owners, per_owner)
    code_of = cluster_of % per_owner * SLOTS + slot_of + 1
    codes = (
        jnp.sum(
            jnp.where(
                position[None, :] == jnp.arange(total, dtype=jnp.int32)[:, None],
                code_of[None, :],
                0,
            ),
            axis=1,
        )
        - 1
    )
    codes = lax.all_to_all(codes.reshape(owners, SEGMENT), "seq", 0, 0, tiled=True)
    packed = pack(position, queries, keys, values, total).reshape(owners, SEGMENT, 3 * row_width)
    rows = lax.all_to_all(packed, "seq", 0, 0, tiled=True).reshape(total, 3 * row_width)
    target, cluster, first = sorted_targets(codes, per_owner)
    first = jnp.pad(first, (0, 128 - per_owner)).reshape(1, 128)
    returned, centroids = attend_clusters(
        target, cluster, first, rows, centroid_sums[0], centroid_counts[0][:, None]
    )
    returned = lax.all_to_all(
        returned.reshape(owners, SEGMENT, row_width), "seq", 0, 0, tiled=True
    ).reshape(total, row_width)
    mixed = lax.psum_scatter(
        project(position, returned, out_weight), "head", scatter_dimension=0, tiled=True
    )
    return (mixed, centroids[None])


def solution(mesh):
    return jax.shard_map(
        shards,
        mesh=mesh,
        in_specs=(
            P("seq", "head"),
            P("seq", "head"),
            P("seq", "head"),
            P("head", "seq"),
            P("head", "seq"),
            P("head", "seq", None),
            P("head", "seq"),
            P("head", None),
        ),
        out_specs=(P(("seq", "head"), None), P("head", "seq", None)),
        check_vma=False,
    )
```

time: 678 us -> 354 us (0.52)
  local copies, waits for them, and re-layouts: 171 us -> 7.84 us
  waiting for transfers between devices: 311 us -> 219 us
  Pallas kernels: 0 us -> 74.9 us
  blocking collectives: 66.9 us -> 0 us
  matrix products: 46.5 us -> 0.39 us
  other arithmetic: 25 us -> 8.73 us
  starting transfers between devices: 35.8 us -> 27.5 us
    all_to_all x3, waiting for transfers between devices: 298 us -> 140 us  [the longest x1 105 us: shards(): lax.all_to_all(packed, 'seq', 0, 0, tiled=True)]
    reshape x5 -> x1, local copies, waits for them, and re-layouts: 82.1 us -> 0.52 us  [shards(): first = jnp.pad(first, (0, 128 - per_owner)).reshape(1, 128)]
    pallas_call x0 -> x3, Pallas kernels: none -> 74.9 us  [the longest x1 41.5 us: attend_clusters(): pl.pallas_call(attend_kernel, in_specs=[vmem] * 7, out_specs=[vmem] * 2,...]
    unnamed x1 -> x0, blocking collectives: 66.9 us -> none
    reduce_scatter x2 -> x1, waiting for transfers between devices: 12.5 us -> 79.1 us  [shards(): lax.psum_scatter(project(position, returned, out_weight), 'head', scatter...]
    dot_general x4 -> x1, matrix products: 46.5 us -> 0.39 us  [block_positions(): before = jnp.dot(belongs, earlier, preferred_element_type=jnp.float32)]
    scatter x2 -> x0, local copies, waits for them, and re-layouts: 28.2 us -> none  [the longest x1 20.7 us: shards(): jnp.zeros((owners * per_owner * SLOTS, 3 * row_width), jnp.bfloat16)]
    another operation x2 -> x1, local copies, waits for them, and re-layouts: 18.2 us -> 0.69 us  [shards(): centroid_counts[0][:, None]]
  transfers between devices with their start and end apart: 5 -> 4, of which waited for: 3 -> 3; matrix products, arithmetic and copies ran while one was open for 22% -> 4% of each run, Pallas kernels for 0% -> 4%
where the time goes in v1:
time: 354 us; the launch traced here: 353 us
  waiting for transfers between devices  219 us (62%)
  Pallas kernels  74.9 us (21%)
  starting transfers between devices  27.5 us (8%)
  between operations  14.2 us (4%)
  other arithmetic  8.73 us (2%)
  local copies, waits for them, and re-layouts  7.84 us (2%)
    all_to_all x1, waiting for transfers between devices, shards(): lax.all_to_all(packed, 'seq', 0, 0, tiled=True)  105 us
    reduce_scatter x1, waiting for transfers between devices, shards(): lax.psum_scatter(project(position, returned, out_weight), 'head', scatter...  79.1 us
    pallas_call x1, Pallas kernels, attend_clusters(): pl.pallas_call(attend_kernel, in_specs=[vmem] * 7, out_specs=[vmem] * 2,...  41.5 us
    all_to_all x1, waiting for transfers between devices, shards(): lax.all_to_all(returned.reshape(owners, SEGMENT, row_width), 'seq', 0, 0,...  35.3 us
    pallas_call x1, Pallas kernels, project(): pl.pallas_call(project_kernel, grid=(columns // OUT_COLS,), in_specs=[pl....  18.1 us
    pallas_call x1, Pallas kernels, pack(): pl.pallas_call(pack_kernel, grid=(rows // PACK_ROWS,), in_specs=[pl.Block...  15.3 us
    all_to_all x1, starting transfers between devices, shards(): lax.all_to_all(returned.reshape(owners, SEGMENT, row_width), 'seq', 0, 0,...  10.2 us
    all_to_all x1, starting transfers between devices, shards(): lax.all_to_all(codes.reshape(owners, SEGMENT), 'seq', 0, 0, tiled=True)  9.59 us
  transfers between devices with their start and end apart: 4, of which 3 were waited for; matrix products, arithmetic and copies ran while one was open for 4% of the time, Pallas kernels for 4%

profile of v1, /device:TPU:1, one launch (start us, length us, event | category | flops | bytes accessed | tf_op | source)
XLA Modules:
  0.0 352.9 jit_solution(9805738943446604659)
XLA Ops:
  7.2 0.7 fusion.17
  7.9 0.4 fusion.2
  8.3 0.7 select_reduce_fusion
  9.1 0.7 sub.25
  9.8 9.6 %all-to-all-start = ((s32[32,1,48]{2,1,0:T(1,128)}), s32[32,1,48]{2,1,0:T(1,128)S(1)}, u32[]{:S(2)}, u32[]{:S(2)}) async-start(s32[32,1,48]{2,1,0:T(1,128)} %sub.25), calls=%async_computation | async-start | bytes 32768 | tf_op jit(solution)/shard_map/all_to_all | solution.py:243
  19.4 15.3 %shard_map.95 = bf16[1536,3072]{1,0:T(8,128)(2,1)} custom-call(s32[1,1024]{1,0:T(1,128)} %copy-done.1, bf16[1024,1024]{1,0:T(8,128)(2,1)} %queries_ref.1, bf16[1024,1024]{1,0:T(8,128)(2,1)} %keys_ref.1, bf16[1024,1024]{1,0:T(8,128)(2,1)} %values_ref.1), custom_call_target="tpu_custom_call" | custom-call | tf_op jit(solution)/shard_map/pallas_call | solution.py:32
  34.7 7.6 %all-to-all-start.1 = ((bf16[32,48,3072]{2,1,0:T(8,128)(2,1)}), bf16[32,48,3072]{2,1,0:T(8,128)(2,1)}, u32[]{:S(2)}, u32[]{:S(2)}) async-start(bf16[32,48,3072]{2,1,0:T(8,128)(2,1)} %bitcast.34), calls=%async_computation.1 | async-start | bytes 18874368 | tf_op jit(solution)/shard_map/all_to_all | solution.py:245
  42.2 0.7 copy.71.counts_ref
  42.9 0.5 broadcast.336
  43.4 1.9 fusion.18
  45.4 0.7 convert_reduce_fusion.1
  46.1 0.1 select_reduce_fusion.3
  46.2 0.2 select_reduce_fusion.2
  46.4 0.2 select_reduce_fusion.1
  46.7 0.4 reduce_sum.76
  47.1 0.4 lt.105
  47.6 0.1 lt.97
  47.7 0.4 rem.105
  48.3 0.5 pad_bitcast_fusion.first_ref
  48.9 0.6 fusion.14
  49.5 1.1 fusion.4.column_target_ref
  50.6 104.9 %all-to-all-done.1 = bf16[32,48,3072]{2,1,0:T(8,128)(2,1)} async-done(((bf16[32,48,3072]{2,1,0:T(8,128)(2,1)}), bf16[32,48,3072]{2,1,0:T(8,128)(2,1)}, u32[]{:S(2)}, u32[]{:S(2)}) %all-to-all-start.1) | async-done | bytes 9437216 | tf_op jit(solution)/shard_map/all_to_all | solution.py:245
  155.5 41.5 %shard_map.96 = (bf16[1536,1024]{1,0:T(8,128)(2,1)}, f32[32,1024]{1,0:T(8,128)}) custom-call(s32[1,1536]{1,0:T(1,128)} %get-tuple-element.14.row_target_ref, s32[1536,1]{1,0:T(8,128)} %fusion.4.column_target_ref, s32[1,1536]{1,0:T(1,128)} %get-tuple-element.13.cluster_ref, s32[1,128]{1,0:T(1,128)} %pad_bitcast_fusion.first_ref, ...), custom_call_target="tpu_custom_call" | custom-call | tf_op jit(solution)/shard_map/pallas_call | solution.py:133
  197.0 10.2 %all-to-all-start.2 = ((bf16[32,48,1024]{2,1,0:T(8,128)(2,1)}), bf16[32,48,1024]{2,1,0:T(8,128)(2,1)S(1)}, u32[]{:S(2)}, u32[]{:S(2)}) async-start(bf16[32,48,1024]{2,1,0:T(8,128)(2,1)} %bitcast.36), calls=%async_computation.2 | async-start | bytes 6291456 | tf_op jit(solution)/shard_map/all_to_all | solution.py:251
  207.2 0.2 reduce-scatter.2.cloned.1.call-start
  207.4 1.0 copy.60
  208.5 1.0 copy.55
  209.5 2.3 fusion.7.position_ref
  211.8 35.3 %all-to-all-done.2 = bf16[32,48,1024]{2,1,0:T(8,128)(2,1)S(1)} async-done(((bf16[32,48,1024]{2,1,0:T(8,128)(2,1)}), bf16[32,48,1024]{2,1,0:T(8,128)(2,1)S(1)}, u32[]{:S(2)}, u32[]{:S(2)}) %all-to-all-start.2) | async-done | bytes 3145760 | tf_op jit(solution)/shard_map/all_to_all | solution.py:251
  247.1 1.8 copy-done
  248.8 18.1 %shard_map.97 = bf16[1024,4096]{1,0:T(8,128)(2,1)} custom-call(s32[1024,1]{1,0:T(8,128)} %fusion.7.position_ref, bf16[1536,1024]{1,0:T(8,128)(2,1)} %bitcast.35, bf16[1024,4096]{1,0:T(8,128)(2,1)} %weight_ref.1), custom_call_target="tpu_custom_call" | custom-call | tf_op jit(solution)/shard_map/pallas_call | solution.py:178
  267.0 79.1 %reduce-scatter.2.cloned.1.call-done = bf16[256,4096]{1,0:T(8,128)(2,1)} async-done(((bf16[1024,4096]{1,0:T(8,128)(2,1)}), bf16[256,4096]{1,0:T(8,128)(2,1)}) %reduce-scatter.2.cloned.1.call-update) | async-done | bytes 2097168 | tf_op jit(solution)/shard_map/reduce_scatter | solution.py:254
  (21 shorter events, 0.4 us)
Async XLA Ops:
  8.3 11.0 %copy-start.1 = (s32[1,1024]{1,0:T(1,128)}, s32[1,1024]{1,0:T(1,128)S(1)}, u32[]{:S(2)}) copy-start(s32[1,1024]{1,0:T(1,128)S(1)} %multiply_add_fusion.position_ref) | copy-start | bytes 12292
  9.8 24.9 %all-to-all-start = ((s32[32,1,48]{2,1,0:T(1,128)}), s32[32,1,48]{2,1,0:T(1,128)S(1)}, u32[]{:S(2)}, u32[]{:S(2)}) async-start(s32[32,1,48]{2,1,0:T(1,128)} %sub.25), calls=%async_computation | async-start | bytes 32768 | tf_op jit(solution)/shard_map/all_to_all | solution.py:243
  34.7 7.6 %copy-start.3 = (f32[1,32]{1,0:T(1,128)S(1)}, f32[1,32]{1,0:T(1,128)}, u32[]{:S(2)}) copy-start(f32[1,32]{1,0:T(1,128)} %param.14) | copy-start | bytes 388
  34.7 120.9 %all-to-all-start.1 = ((bf16[32,48,3072]{2,1,0:T(8,128)(2,1)}), bf16[32,48,3072]{2,1,0:T(8,128)(2,1)}, u32[]{:S(2)}, u32[]{:S(2)}) async-start(bf16[32,48,3072]{2,1,0:T(8,128)(2,1)} %bitcast.34), calls=%async_computation.1 | async-start | bytes 18874368 | tf_op jit(solution)/shard_map/all_to_all | solution.py:245
  155.5 52.9 %copy-start.2 = (s32[1,1024]{1,0:T(1,128)S(1)}, s32[1,1024]{1,0:T(1,128)}, u32[]{:S(2)}) copy-start(s32[1,1024]{1,0:T(1,128)} %param.11) | copy-start | bytes 12292
  197.0 50.0 %all-to-all-start.2 = ((bf16[32,48,1024]{2,1,0:T(8,128)(2,1)}), bf16[32,48,1024]{2,1,0:T(8,128)(2,1)S(1)}, u32[]{:S(2)}, u32[]{:S(2)}) async-start(bf16[32,48,1024]{2,1,0:T(8,128)(2,1)} %bitcast.36), calls=%async_computation.2 | async-start | bytes 6291456 | tf_op jit(solution)/shard_map/all_to_all | solution.py:251
  207.2 138.9 %reduce-scatter.2.cloned.1.call-start = ((), (), s32[]{:S(2)}) async-start(), calls=%async_computation.4 | async-start | bytes 10485760 | tf_op jit(solution)/shard_map/reduce_scatter | solution.py:254
  247.1 1.8 copy-start
Sparse Core Ops, SparseCore 0:
  267.1 78.9 reduce-scatter.1

commit v2 on v1

v2 whole, which is shorter than its diff:
```python
import jax
import jax.numpy as jnp
from jax import lax
from jax.experimental import pallas as pl
from jax.experimental.pallas import tpu as pltpu
from jax.sharding import PartitionSpec as P

HD = 128
SLOTS = 3
SEGMENT = 48
TILE = 128
PACK_ROWS = 384
OUT_COLS = 512
HALVES = 2
NEG = -1e30

VMEM = pl.BlockSpec(memory_space=pltpu.VMEM)
BIG = pltpu.CompilerParams(vmem_limit_bytes=60 << 20)


def cost(flops, moved):
    return pl.CostEstimate(flops=flops, bytes_accessed=moved, transcendentals=0)


def pack_kernel(position_ref, values_ref, packed_ref):
    rows, tokens = packed_ref.shape[0], values_ref.shape[0]
    first = pl.program_id(0) * rows
    row_of = first + lax.broadcasted_iota(jnp.int32, (rows, tokens), 0)
    pick = (row_of == position_ref[...]).astype(jnp.bfloat16)
    packed_ref[...] = jnp.dot(
        pick, values_ref[...], preferred_element_type=jnp.float32
    ).astype(jnp.bfloat16)


def pack(position, values, rows):
    tokens, width = values.shape
    return pl.pallas_call(
        pack_kernel,
        grid=(rows // PACK_ROWS,),
        in_specs=[
            pl.BlockSpec((1, tokens), lambda i: (0, 0)),
            pl.BlockSpec((tokens, width), lambda i: (0, 0)),
        ],
        out_specs=pl.BlockSpec((PACK_ROWS, width), lambda i: (i, 0)),
        out_shape=jax.ShapeDtypeStruct((rows, width), jnp.bfloat16),
        cost_estimate=cost(2 * rows * tokens * width, 2 * width * (rows + tokens)),
    )(position.reshape(1, tokens), values)


def order_rows(target_ref, rows_ref, ordered_ref, offset):
    rows = rows_ref.shape[0]

    def order(step, carry):
        start = step * (2 * TILE)
        place = start + lax.broadcasted_iota(jnp.int32, (2 * TILE, rows), 0)
        pick = (place == target_ref[...]).astype(jnp.bfloat16)
        ordered_ref[pl.ds(start + offset, 2 * TILE), :] = jnp.dot(
            pick, rows_ref[...], preferred_element_type=jnp.float32
        ).astype(jnp.bfloat16)
        return carry

    lax.fori_loop(0, rows // (2 * TILE), order, 0)


def keys_kernel(target_ref, cluster_ref, rows_ref, sums_ref, counts_ref, ordered_ref, centroids_ref):
    rows, width = rows_ref.shape
    clusters = sums_ref.shape[0]
    belongs = lax.broadcasted_iota(jnp.int32, (clusters, rows), 0) == cluster_ref[...]
    batch_sums = jnp.dot(
        belongs.astype(jnp.bfloat16), rows_ref[...], preferred_element_type=jnp.float32
    )
    batch_counts = jnp.sum(belongs.astype(jnp.float32), axis=1, keepdims=True)
    centroids_ref[...] = (0.6 * sums_ref[...] + 0.4 * batch_sums) / (
        0.6 * counts_ref[...] + 0.4 * batch_counts
    )
    ordered_ref[0:TILE, :] = jnp.zeros((TILE, width), jnp.bfloat16)
    order_rows(target_ref, rows_ref, ordered_ref, TILE)


def order_keys(target, cluster, rows, sums, counts):
    total, width = rows.shape
    return pl.pallas_call(
        keys_kernel,
        in_specs=[VMEM] * 5,
        out_specs=[VMEM] * 2,
        out_shape=[
            jax.ShapeDtypeStruct((total + TILE, width), jnp.bfloat16),
            jax.ShapeDtypeStruct(sums.shape, jnp.float32),
        ],
        compiler_params=BIG,
        cost_estimate=cost(2 * total * total * width, 4 * total * width),
    )(target.reshape(1, total), cluster.reshape(1, total), rows, sums, counts)


def weights_kernel(target_ref, first_ref, keys_ref, rows_ref, weights_ref, ordered_ref):
    heads, rows = weights_ref.shape[:2]
    order_rows(target_ref, rows_ref, ordered_ref, 0)

    def score(step, carry):
        start = step * TILE
        place = start + lax.broadcasted_iota(jnp.int32, (TILE, first_ref.shape[1]), 0)
        first = first_ref[...]
        low = jnp.max(jnp.where(first <= place, first, 0), axis=1, keepdims=True)
        query_place = start + lax.broadcasted_iota(jnp.int32, (TILE, 2 * TILE), 0)
        key_place = start - TILE + lax.broadcasted_iota(jnp.int32, (TILE, 2 * TILE), 1)
        seen = (key_place <= query_place) & (key_place >= low)
        for head in range(heads):
            column = head * HD
            query = ordered_ref[pl.ds(start, TILE), column : column + HD]
            key = keys_ref[pl.ds(start, 2 * TILE), column : column + HD]
            scores = lax.dot_general(
                query, key, (((1,), (1,)), ((), ())), preferred_element_type=jnp.float32
            ) * (HD**-0.5)
            scores = jnp.where(seen, scores, NEG)
            shifted = jnp.exp(scores - jnp.max(scores, axis=1, keepdims=True))
            weights = shifted / jnp.sum(shifted, axis=1, keepdims=True)
            weights_ref[head, pl.ds(start, TILE), :] = weights.astype(jnp.bfloat16)
        return carry

    lax.fori_loop(0, rows // TILE, score, 0)


def attention_weights(target, first, keys, rows):
    total, width = rows.shape
    heads = width // HD
    return pl.pallas_call(
        weights_kernel,
        in_specs=[VMEM] * 4,
        out_specs=VMEM,
        out_shape=jax.ShapeDtypeStruct((heads, total, 2 * TILE), jnp.bfloat16),
        scratch_shapes=[pltpu.VMEM((total, width), jnp.bfloat16)],
        compiler_params=BIG,
        cost_estimate=cost(4 * total * total * width, 8 * total * width),
    )(target.reshape(1, total), first, keys, rows)


def attend_kernel(
    row_target_ref, column_target_ref, weights_ref, rows_ref, returned_ref, ordered_ref, attended_ref
):
    rows, width = rows_ref.shape
    ordered_ref[0:TILE, :] = jnp.zeros((TILE, width), jnp.bfloat16)
    order_rows(row_target_ref, rows_ref, ordered_ref, TILE)

    def attend(step, carry):
        start = step * TILE
        for head in range(width // HD):
            column = head * HD
            value = ordered_ref[pl.ds(start, 2 * TILE), column : column + HD]
            attended_ref[pl.ds(start, TILE), column : column + HD] = jnp.dot(
                weights_ref[head, pl.ds(start, TILE), :],
                value,
                preferred_element_type=jnp.float32,
            ).astype(jnp.bfloat16)
        return carry

    lax.fori_loop(0, rows // TILE, attend, 0)

    def restore(step, carry):
        start = step * (2 * TILE)
        target = column_target_ref[pl.ds(start, 2 * TILE), :]
        pick = (lax.broadcasted_iota(jnp.int32, (2 * TILE, rows), 1) == target).astype(jnp.bfloat16)
        returned_ref[pl.ds(start, 2 * TILE), :] = jnp.dot(
            pick, attended_ref[...], preferred_element_type=jnp.float32
        ).astype(jnp.bfloat16)
        return carry

    lax.fori_loop(0, rows // (2 * TILE), restore, 0)


def attend_half(half, target, weights, rows):
    total, width = rows.shape
    heads, part = weights.shape[0] // HALVES, width // HALVES
    return pl.pallas_call(
        attend_kernel,
        grid=(1,),
        in_specs=[
            pl.BlockSpec((1, total), lambda i: (0, 0)),
            pl.BlockSpec((total, 1), lambda i: (0, 0)),
            pl.BlockSpec((heads, total, 2 * TILE), lambda i: (half, 0, 0)),
            pl.BlockSpec((total, part), lambda i: (0, half)),
        ],
        out_specs=pl.BlockSpec((total, part), lambda i: (0, 0)),
        out_shape=jax.ShapeDtypeStruct((total, part), jnp.bfloat16),
        scratch_shapes=[
            pltpu.VMEM((total + TILE, part), jnp.bfloat16),
            pltpu.VMEM((total, part), jnp.bfloat16),
        ],
        compiler_params=BIG,
        cost_estimate=cost(4 * total * total * part, 8 * total * part),
    )(target.reshape(1, total), target.reshape(total, 1), weights, rows)


def unpack_kernel(position_ref, rows_ref, *out_refs):
    quarter, total = out_refs[0].shape[0], rows_ref.shape[0]
    for index, out_ref in enumerate(out_refs):
        position = position_ref[index * quarter : (index + 1) * quarter, :]
        pick = (lax.broadcasted_iota(jnp.int32, (quarter, total), 1) == position).astype(
            jnp.bfloat16
        )
        out_ref[...] = jnp.dot(pick, rows_ref[...], preferred_element_type=jnp.float32).astype(
            jnp.bfloat16
        )


def unpack(position, rows, parts):
    tokens = position.shape[0]
    total, width = rows.shape
    return pl.pallas_call(
        unpack_kernel,
        in_specs=[VMEM] * 2,
        out_specs=[VMEM] * parts,
        out_shape=[jax.ShapeDtypeStruct((tokens // parts, width), jnp.bfloat16)] * parts,
        cost_estimate=cost(2 * tokens * total * width, 2 * width * (total + tokens)),
    )(position.reshape(tokens, 1), rows)


def project_kernel(core_ref, *refs):
    groups = (len(refs) - 1) // (HALVES + 2)
    row_refs = refs[: groups * HALVES]
    own_ref = refs[groups * HALVES]
    weight_refs = refs[groups * HALVES + 1 : -2]
    out_ref, rows_ref = refs[-2:]
    part = row_refs[0].shape[1]
    width = part * HALVES
    step = pl.program_id(0)

    @pl.when(step == 0)
    def _():
        for index, ref in enumerate(row_refs):
            rows_ref[:, index * part : (index + 1) * part] = ref[...]

    def product(side):
        total = jnp.dot(rows_ref[:, :width], own_ref[...], preferred_element_type=jnp.float32)
        for index, ref in enumerate(weight_refs[side * (groups - 1) : (side + 1) * (groups - 1)]):
            total += jnp.dot(
                rows_ref[:, (index + 1) * width : (index + 2) * width],
                ref[...],
                preferred_element_type=jnp.float32,
            )
        out_ref[...] = total.astype(jnp.bfloat16)

    steps = pl.num_programs(0)

    @pl.when(step < steps // 2)
    def _():
        product(0)

    @pl.when(step >= steps // 2)
    def _():
        product(1)


def project(core, rows, own, near, far):
    tokens, part = rows[0].shape
    width, columns = own.shape
    groups = len(near) + 1
    steps = columns // OUT_COLS
    middle = steps // 2
    placed = lambda i, core: (0, lax.rem(core[0] * middle + i, steps))
    return pl.pallas_call(
        project_kernel,
        grid_spec=pltpu.PrefetchScalarGridSpec(
            num_scalar_prefetch=1,
            grid=(steps,),
            in_specs=[pl.BlockSpec((tokens, part), lambda i, core: (0, 0))] * len(rows)
            + [pl.BlockSpec((width, OUT_COLS), placed)]
            + [pl.BlockSpec((width, OUT_COLS), lambda i, core: (0, jnp.minimum(i, middle - 1)))]
            * len(near)
            + [pl.BlockSpec((width, OUT_COLS), lambda i, core: (0, jnp.maximum(i - middle, 0)))]
            * len(far),
            out_specs=pl.BlockSpec((tokens, OUT_COLS), placed),
            scratch_shapes=[pltpu.VMEM((tokens, groups * width), jnp.bfloat16)],
        ),
        out_shape=jax.ShapeDtypeStruct((tokens, columns), jnp.bfloat16),
        compiler_params=BIG,
        cost_estimate=cost(2 * tokens * groups * width * columns, 2 * groups * width * columns),
    )(core, *rows, own, *near, *far)


def block_positions(cluster_of, owners, per_owner):
    tokens = cluster_of.shape[0]
    owner_of = cluster_of // per_owner
    belongs = (jnp.arange(owners, dtype=jnp.int32)[:, None] == owner_of[None, :]).astype(
        jnp.bfloat16
    )
    token = jnp.arange(tokens, dtype=jnp.int32)
    earlier = (token[:, None] < token[None, :]).astype(jnp.bfloat16)
    before = jnp.dot(belongs, earlier, preferred_element_type=jnp.float32)
    rank = jnp.sum(before * belongs.astype(jnp.float32), axis=0)
    return owner_of * SEGMENT + rank.astype(jnp.int32)


def sorted_targets(codes, per_owner):
    owners = codes.shape[0]
    cluster = jnp.where(codes < 0, -1, codes // SLOTS)
    slot = codes % SLOTS
    here = jnp.arange(per_owner, dtype=jnp.int32)
    one_hot = (cluster[:, :, None] == here[None, None, :]).astype(jnp.int32)
    count = jnp.sum(one_hot, axis=1)
    source = jnp.arange(owners, dtype=jnp.int32)
    before = jnp.sum(
        jnp.where((source[None, :] < source[:, None])[:, :, None], count[None, :, :], 0), axis=1
    )
    total = jnp.sum(count, axis=0)
    first = jnp.sum(jnp.where(here[None, :] < here[:, None], total[None, :], 0), axis=1)
    base = first[None, :] + before
    target = jnp.sum(one_hot * base[:, None, :], axis=2) + slot
    return jnp.where(codes < 0, -1, target), cluster, first


def exchange(rows, owners):
    width = rows.shape[1]
    rows = lax.all_to_all(rows.reshape(owners, SEGMENT, width), "seq", 0, 0, tiled=True)
    return rows.reshape(owners * SEGMENT, width)


def shards(queries, keys, values, cluster_ids, slots, centroid_sums, centroid_counts, out_weight):
    owners = lax.axis_size("seq")
    groups = lax.axis_size("head")
    tokens = queries.shape[0]
    columns = out_weight.shape[1]
    per_owner = centroid_sums.shape[1]
    total = owners * SEGMENT
    cluster_of = cluster_ids[0]
    slot_of = slots[0]
    core = lax.axis_index("seq") % 2
    group = lax.axis_index("head")

    def shift(value, by):
        return lax.ppermute(value, "head", [(i, (i + by) % groups) for i in range(groups)])

    def swap(value):
        return lax.ppermute(value, "seq", [(i, i ^ 1) for i in range(owners)])

    position = block_positions(cluster_of, owners, per_owner)
    packed_keys = pack(position, keys, total)
    rows_keys = exchange(packed_keys, owners)

    position_later, _ = lax.optimization_barrier((position, packed_keys))
    half_weight = lax.dynamic_slice_in_dim(out_weight, core * (columns // 2), columns // 2, 1)
    near = [shift(half_weight, by) for by in range(1, groups)]
    far = [swap(value) for value in near]

    code_of = cluster_of % per_owner * SLOTS + slot_of + 1
    codes = (
        jnp.sum(
            jnp.where(
                position_later[None, :] == jnp.arange(total, dtype=jnp.int32)[:, None],
                code_of[None, :],
                0,
            ),
            axis=1,
        )
        - 1
    )
    codes = lax.all_to_all(codes.reshape(owners, SEGMENT), "seq", 0, 0, tiled=True)
    rows_queries = exchange(pack(position_later, queries, total), owners)
    rows_values = exchange(pack(position_later, values, total), owners)

    target, cluster, first = sorted_targets(codes, per_owner)
    first = jnp.pad(first, (0, 128 - per_owner)).reshape(1, 128)
    ordered_keys, centroids = order_keys(
        target, cluster, rows_keys, centroid_sums[0], centroid_counts[0][:, None]
    )
    weights = attention_weights(target, first, ordered_keys, rows_queries)

    quarter = jnp.arange(groups, dtype=jnp.int32)
    rolled = position.reshape(groups, tokens // groups)[(group + quarter) % groups].reshape(tokens)
    halves = []
    for half in range(HALVES):
        returned = exchange(attend_half(half, target, weights, rows_values), owners)
        pieces = unpack(rolled, returned, groups)
        halves.append([pieces[0]] + [shift(pieces[by], by) for by in range(1, groups)])
    rows = [halves[half][by] for by in range(groups) for half in range(HALVES)]
    mixed = project(core.reshape(1), rows, out_weight, near, far)
    return (mixed, centroids[None])


def solution(mesh):
    return jax.shard_map(
        shards,
        mesh=mesh,
        in_specs=(
            P("seq", "head"),
            P("seq", "head"),
            P("seq", "head"),
            P("head", "seq"),
            P("head", "seq"),
            P("head", "seq", None),
            P("head", "seq"),
            P("head", None),
        ),
        out_specs=(P(("seq", "head"), None), P("head", "seq", None)),
        check_vma=False,
    )
```

time: 354 us -> 409 us (1.16)
  Pallas kernels: 74.9 us -> 103 us
  blocking collectives: 0 us -> 16.4 us
  between operations: 14.2 us -> 0.91 us
  starting transfers between devices: 27.5 us -> 39.5 us
  local copies, waits for them, and re-layouts: 7.84 us -> 15.1 us
    ppermute x0 -> x12, waiting for transfers between devices: none -> 143 us  [the longest x9 143 us: shift(): lax.ppermute(value, 'head', [(i, (i + by) % groups) for i in range(groups)])]
    reduce_scatter x1 -> x0, waiting for transfers between devices: 79.1 us -> none  [shards(): lax.psum_scatter(project(position, returned, out_weight), 'head', scatter...]
    all_to_all x3 -> x5, waiting for transfers between devices: 140 us -> 78.2 us  [exchange(): lax.all_to_all(rows.reshape(owners, SEGMENT, width), 'seq', 0, 0, tiled=T...]
    pallas_call x2 -> x7, Pallas kernels: 59.6 us -> 83.3 us  [the longest x2 27.4 us: attend_half(): pl.pallas_call(attend_kernel, grid=(1,), in_specs=[pl.BlockSpec((1, total...]
    all_to_all x0 -> x1, blocking collectives: none -> 16.4 us  [shards(): lax.all_to_all(codes.reshape(owners, SEGMENT), 'seq', 0, 0, tiled=True)]
    ppermute x0 -> x12, starting transfers between devices: none -> 9.27 us  [the longest x9 7.39 us: shift(): lax.ppermute(value, 'head', [(i, (i + by) % groups) for i in range(groups)])]
    dynamic_slice x0 -> x1, local copies, waits for them, and re-layouts: none -> 4.75 us  [shards(): lax.dynamic_slice_in_dim(out_weight, core * (columns // 2), columns // 2, 1)]
    pallas_call x1 -> x3, Pallas kernels: 15.3 us -> 19.5 us  [pack(): pl.pallas_call(pack_kernel, grid=(rows // PACK_ROWS,), in_specs=[pl.Block...]
  transfers between devices with their start and end apart: 4 -> 17, of which waited for: 3 -> 10; matrix products, arithmetic and copies ran while one was open for 4% -> 4% of each run, Pallas kernels for 4% -> 19%
where the time goes in v2:
time: 409 us; the launch traced here: 406 us
  waiting for transfers between devices  221 us (54%)
  Pallas kernels  103 us (25%)
  starting transfers between devices  39.5 us (10%)
  blocking collectives  16.4 us (4%)
  local copies, waits for them, and re-layouts  15.1 us (4%)
  other arithmetic  9.7 us (2%)
    ppermute x9, waiting for transfers between devices, shift(): lax.ppermute(value, 'head', [(i, (i + by) % groups) for i in range(groups)])  143 us
    all_to_all x5, waiting for transfers between devices, exchange(): lax.all_to_all(rows.reshape(owners, SEGMENT, width), 'seq', 0, 0, tiled=T...  78.2 us
    all_to_all x5, starting transfers between devices, exchange(): lax.all_to_all(rows.reshape(owners, SEGMENT, width), 'seq', 0, 0, tiled=T...  30.3 us
    pallas_call x2, Pallas kernels, attend_half(): pl.pallas_call(attend_kernel, grid=(1,), in_specs=[pl.BlockSpec((1, total...  27.4 us
    pallas_call x3, Pallas kernels, pack(): pl.pallas_call(pack_kernel, grid=(rows // PACK_ROWS,), in_specs=[pl.Block...  19.5 us
    pallas_call x1, Pallas kernels, project(): pl.pallas_call(project_kernel, grid_spec=pltpu.PrefetchScalarGridSpec(num...  18.8 us
    pallas_call x1, Pallas kernels, attention_weights(): pl.pallas_call(weights_kernel, in_specs=[VMEM] * 4, out_specs=VMEM, out_s...  18.6 us
    all_to_all x1, blocking collectives, shards(): lax.all_to_all(codes.reshape(owners, SEGMENT), 'seq', 0, 0, tiled=True)  16.4 us
  transfers between devices with their start and end apart: 17, of which 10 were waited for; matrix products, arithmetic and copies ran while one was open for 4% of the time, Pallas kernels for 19%

profile of v2, /device:TPU:1, one launch (start us, length us, event | category | flops | bytes accessed | tf_op | source)
XLA Modules:
  0.0 405.6 jit_solution(15013166198215299187)
XLA Ops:
  4.3 6.5 %shard_map.95 = bf16[1536,1024]{1,0:T(8,128)(2,1)} custom-call(s32[1,1024]{1,0:T(1,128)} %multiply_add_fusion.position_ref, bf16[1024,1024]{1,0:T(8,128)(2,1)} %values_ref.3), custom_call_target="tpu_custom_call" | custom-call | flops 3221225472 | bytes 5242880 | tf_op jit(solution)/shard_map/pallas_call | solution.py:37
  11.5 16.4 %all_to_all.31 = s32[32,1,48]{2,1,0:T(1,128)S(1)} all-to-all(s32[32,1,48]{2,1,0:T(1,128)S(1)} %sub.28), channel_id=1, replica_groups=mesh['seq'=32,'head'=4] {'seq'}, dimensions={0} | all-to-all | bytes 12288 | tf_op jit(solution)/shard_map/all_to_all | solution.py:356
  27.9 4.4 %all-to-all-start.1 = ((bf16[32,48,1024]{2,1,0:T(8,128)(2,1)}), bf16[32,48,1024]{2,1,0:T(8,128)(2,1)S(1)}, u32[]{:S(2)}, u32[]{:S(2)}) async-start(bf16[32,48,1024]{2,1,0:T(8,128)(2,1)} %bitcast.50), calls=%async_computation.1 | async-start | bytes 6291456 | tf_op jit(solution)/shard_map/all_to_all | solution.py:313
  32.3 6.6 %shard_map.97 = bf16[1536,1024]{1,0:T(8,128)(2,1)} custom-call(s32[1,1024]{1,0:T(1,128)} %bitcast.66, bf16[1024,1024]{1,0:T(8,128)(2,1)} %values_ref.4), custom_call_target="tpu_custom_call" | custom-call | flops 3221225472 | bytes 5242880 | tf_op jit(solution)/shard_map/pallas_call | solution.py:37
  38.8 33.3 %all-to-all-done.1 = bf16[32,48,1024]{2,1,0:T(8,128)(2,1)S(1)} async-done(((bf16[32,48,1024]{2,1,0:T(8,128)(2,1)}), bf16[32,48,1024]{2,1,0:T(8,128)(2,1)S(1)}, u32[]{:S(2)}, u32[]{:S(2)}) %all-to-all-start.1) | async-done | bytes 3145760 | tf_op jit(solution)/shard_map/all_to_all | solution.py:313
  72.1 1.7 copy-done.1
  73.8 6.2 %all-to-all-start.2 = ((bf16[32,48,1024]{2,1,0:T(8,128)(2,1)}), bf16[32,48,1024]{2,1,0:T(8,128)(2,1)S(1)}, u32[]{:S(2)}, u32[]{:S(2)}) async-start(bf16[32,48,1024]{2,1,0:T(8,128)(2,1)} %bitcast.49), calls=%async_computation.2 | async-start | bytes 6291456 | tf_op jit(solution)/shard_map/all_to_all | solution.py:313
  80.1 4.7 %constant_dynamic-slice_fusion = bf16[1024,2048]{1,0:T(8,128)(2,1)} fusion(bf16[1024,4096]{1,0:T(8,128)(2,1)} %refs_8_.1, s32[]{:T(128)S(6)} %select_n.158), kind=kLoop, calls=%fused_computation.67 | loop fusion | bytes 8388612 | tf_op jit(solution)/shard_map/dynamic_slice | solution.py:340
  84.8 2.5 collective-permute-start.8
  89.1 6.5 %shard_map.99 = bf16[1536,1024]{1,0:T(8,128)(2,1)} custom-call(s32[1,1024]{1,0:T(1,128)} %bitcast.67, bf16[1024,1024]{1,0:T(8,128)(2,1)} %values_ref.5), custom_call_target="tpu_custom_call" | custom-call | flops 3221225472 | bytes 5242880 | tf_op jit(solution)/shard_map/pallas_call | solution.py:37
  95.6 1.9 fusion.24
  98.5 21.4 %all-to-all-done.2 = bf16[32,48,1024]{2,1,0:T(8,128)(2,1)S(1)} async-done(((bf16[32,48,1024]{2,1,0:T(8,128)(2,1)}), bf16[32,48,1024]{2,1,0:T(8,128)(2,1)S(1)}, u32[]{:S(2)}, u32[]{:S(2)}) %all-to-all-start.2) | async-done | bytes 3145760 | tf_op jit(solution)/shard_map/all_to_all | solution.py:313
  119.9 6.9 %all-to-all-start.3 = ((bf16[32,48,1024]{2,1,0:T(8,128)(2,1)}), bf16[32,48,1024]{2,1,0:T(8,128)(2,1)}, u32[]{:S(2)}, u32[]{:S(2)}) async-start(bf16[32,48,1024]{2,1,0:T(8,128)(2,1)} %bitcast.48), calls=%async_computation.3 | async-start | bytes 6291456 | tf_op jit(solution)/shard_map/all_to_all | solution.py:313
  131.7 2.5 fusion.4.column_target_ref
  134.2 10.2 %shard_map.96 = (bf16[1664,1024]{1,0:T(8,128)(2,1)}, f32[32,1024]{1,0:T(8,128)}) custom-call(s32[1,1536]{1,0:T(1,128)} %get-tuple-element.32.target_ref.row_target_ref, s32[1,1536]{1,0:T(1,128)} %get-tuple-element.31.cluster_ref, bf16[1536,1024]{1,0:T(8,128)(2,1)} %bitcast.47, f32[32,1024]{1,0:T(8,128)} %bitcast.70, f32[32,1]{1,0:T(8,128)} %copy.43.counts_ref), custom_call_target="tpu_custom_call" | custom-call | flops 4831838208 | bytes 6291456 | tf_op jit(solution)/shard_map/pallas_call | solution.py:82
  144.4 122.5 %collective-permute-done.8.refs_11_ = bf16[1024,2048]{1,0:T(8,128)(2,1)} collective-permute-done((bf16[1024,2048]{1,0:T(8,128)(2,1)}, bf16[1024,2048]{1,0:T(8,128)(2,1)}, u32[]{:S(2)}, u32[]{:S(2)}) %collective-permute-start.8) | collective-permute-done | bytes 4194336 | tf_op jit(solution)/shard_map/ppermute | solution.py:330
  266.9 1.4 collective-permute-start.11
  268.3 3.2 collective-permute-done.6.refs_9_
  272.0 18.6 %shard_map.98.weights_ref = bf16[8,1536,256]{2,1,0:T(8,128)(2,1)} custom-call(s32[1,1536]{1,0:T(1,128)} %get-tuple-element.32.target_ref.row_target_ref, s32[1,128]{1,0:T(1,128)} %pad_bitcast_fusion.first_ref, bf16[1664,1024]{1,0:T(8,128)(2,1)} %get-tuple-element.14.keys_ref, bf16[1536,1024]{1,0:T(8,128)(2,1)} %bitcast.46), custom_call_target="tpu_custom_call" | custom-call | flops 9663676416 | bytes 12582912 | tf_op jit(solution)/shard_map/pallas_call | solution.py:126
  290.5 13.7 %shard_map.100 = bf16[1536,512]{1,0:T(8,128)(2,1)} custom-call(s32[1,1536]{1,0:T(1,128)} %get-tuple-element.32.target_ref.row_target_ref, s32[1536,1]{1,0:T(8,128)} %fusion.4.column_target_ref, bf16[8,1536,256]{2,1,0:T(8,128)(2,1)} %shard_map.98.weights_ref, bf16[1536,1024]{1,0:T(8,128)(2,1)} %bitcast.22.rows_ref), custom_call_target="tpu_custom_call" | custom-call | flops 4831838208 | bytes 6291456 | tf_op jit(solution)/shard_map/pallas_call | solution.py:173
  304.2 7.2 %all-to-all-start.4 = ((bf16[32,48,512]{2,1,0:T(8,128)(2,1)}), bf16[32,48,512]{2,1,0:T(8,128)(2,1)S(1)}, u32[]{:S(2)}, u32[]{:S(2)}) async-start(bf16[32,48,512]{2,1,0:T(8,128)(2,1)} %bitcast.54), calls=%async_computation.4 | async-start | bytes 3145728 | tf_op jit(solution)/shard_map/all_to_all | solution.py:313
  311.5 13.7 %shard_map.102 = bf16[1536,512]{1,0:T(8,128)(2,1)} custom-call(s32[1,1536]{1,0:T(1,128)} %get-tuple-element.32.target_ref.row_target_ref, s32[1536,1]{1,0:T(8,128)} %fusion.4.column_target_ref, bf16[8,1536,256]{2,1,0:T(8,128)(2,1)} %shard_map.98.weights_ref, bf16[1536,1024]{1,0:T(8,128)(2,1)} %bitcast.22.rows_ref), custom_call_target="tpu_custom_call" | custom-call | flops 4831838208 | bytes 6291456 | tf_op jit(solution)/shard_map/pallas_call | solution.py:173
  325.2 8.5 %all-to-all-done.4 = bf16[32,48,512]{2,1,0:T(8,128)(2,1)S(1)} async-done(((bf16[32,48,512]{2,1,0:T(8,128)(2,1)}), bf16[32,48,512]{2,1,0:T(8,128)(2,1)S(1)}, u32[]{:S(2)}, u32[]{:S(2)}) %all-to-all-start.4) | async-done | bytes 1572896 | tf_op jit(solution)/shard_map/all_to_all | solution.py:313
  333.7 5.6 %all-to-all-start.5 = ((bf16[32,48,512]{2,1,0:T(8,128)(2,1)}), bf16[32,48,512]{2,1,0:T(8,128)(2,1)S(1)}, u32[]{:S(2)}, u32[]{:S(2)}) async-start(bf16[32,48,512]{2,1,0:T(8,128)(2,1)} %bitcast.51), calls=%async_computation.5 | async-start | bytes 3145728 | tf_op jit(solution)/shard_map/all_to_all | solution.py:313
  340.9 4.1 %shard_map.101 = (bf16[256,512]{1,0:T(8,128)(2,1)}, bf16[256,512]{1,0:T(8,128)(2,1)}, bf16[256,512]{1,0:T(8,128)(2,1)}, bf16[256,512]{1,0:T(8,128)(2,1)}) custom-call(s32[1024,1]{1,0:T(8,128)} %bitcast.55, bf16[1536,512]{1,0:T(8,128)(2,1)} %bitcast.53), custom_call_target="tpu_custom_call" | custom-call | flops 1610612736 | bytes 2621440 | tf_op jit(solution)/shard_map/pallas_call | solution.py:208
  345.1 1.6 collective-permute-start.2
  346.6 15.0 %all-to-all-done.5 = bf16[32,48,512]{2,1,0:T(8,128)(2,1)S(1)} async-done(((bf16[32,48,512]{2,1,0:T(8,128)(2,1)}), bf16[32,48,512]{2,1,0:T(8,128)(2,1)S(1)}, u32[]{:S(2)}, u32[]{:S(2)}) %all-to-all-start.5) | async-done | bytes 1572896 | tf_op jit(solution)/shard_map/all_to_all | solution.py:313
  362.7 4.2 %shard_map.103 = (bf16[256,512]{1,0:T(8,128)(2,1)}, bf16[256,512]{1,0:T(8,128)(2,1)}, bf16[256,512]{1,0:T(8,128)(2,1)}, bf16[256,512]{1,0:T(8,128)(2,1)}) custom-call(s32[1024,1]{1,0:T(8,128)} %bitcast.56, bf16[1536,512]{1,0:T(8,128)(2,1)} %bitcast.52), custom_call_target="tpu_custom_call" | custom-call | flops 1610612736 | bytes 2621440 | tf_op jit(solution)/shard_map/pallas_call | solution.py:208
  368.4 4.5 %collective-permute-done.4.refs_6_ = bf16[256,512]{1,0:T(8,128)(2,1)S(1)} collective-permute-done((bf16[256,512]{1,0:T(8,128)(2,1)S(1)}, bf16[256,512]{1,0:T(8,128)(2,1)S(1)}, u32[]{:S(2)}, u32[]{:S(2)}) %collective-permute-start.4) | collective-permute-done | bytes 262176 | tf_op jit(solution)/shard_map/ppermute | solution.py:330
  374.6 5.2 %collective-permute-done.3.refs_5_ = bf16[256,512]{1,0:T(8,128)(2,1)S(1)} collective-permute-done((bf16[256,512]{1,0:T(8,128)(2,1)}, bf16[256,512]{1,0:T(8,128)(2,1)S(1)}, u32[]{:S(2)}, u32[]{:S(2)}) %collective-permute-start.3) | collective-permute-done | bytes 262176 | tf_op jit(solution)/shard_map/ppermute | solution.py:330
  379.8 6.2 %collective-permute-done.5.refs_7_ = bf16[256,512]{1,0:T(8,128)(2,1)S(1)} collective-permute-done((bf16[256,512]{1,0:T(8,128)(2,1)}, bf16[256,512]{1,0:T(8,128)(2,1)S(1)}, u32[]{:S(2)}, u32[]{:S(2)}) %collective-permute-start.5) | collective-permute-done | bytes 262176 | tf_op jit(solution)/shard_map/ppermute | solution.py:330
  386.7 18.8 %shard_map.104 = bf16[256,4096]{1,0:T(8,128)(2,1)} custom-call(s32[1]{0:T(128)} %bitcast.core_ref, bf16[256,512]{1,0:T(8,128)(2,1)} %get-tuple-element.15.refs_0_, bf16[256,512]{1,0:T(8,128)(2,1)} %get-tuple-element.16.refs_1_, bf16[256,512]{1,0:T(8,128)(2,1)} %copy-done.4, bf16[256,512]{1,0:T(8,128)(2,1)} %copy-done.7, bf16[256,512]{1,0:T(8,128)(2,1)} %copy-done.5, ...), custom_call_target="tpu_custom_call" | custom-call | flops 8589934592 | bytes 33554432 | tf_op jit(solution)/shard_map/pallas_call | solution.py:260
  (79 shorter events, 19.3 us)
Async XLA Ops:
  3.7 7.1 %copy-start.10 = (s32[1024]{0:T(1024)}, s32[1024]{0:T(1024)S(1)}, u32[]{:S(2)}) copy-start(s32[1024]{0:T(1024)S(1)} %fusion.16) | copy-start | bytes 12292
  27.9 44.2 %all-to-all-start.1 = ((bf16[32,48,1024]{2,1,0:T(8,128)(2,1)}), bf16[32,48,1024]{2,1,0:T(8,128)(2,1)S(1)}, u32[]{:S(2)}, u32[]{:S(2)}) async-start(bf16[32,48,1024]{2,1,0:T(8,128)(2,1)} %bitcast.50), calls=%async_computation.1 | async-start | bytes 6291456 | tf_op jit(solution)/shard_map/all_to_all | solution.py:313
  72.1 1.7 copy-start.1
  73.8 46.1 %all-to-all-start.2 = ((bf16[32,48,1024]{2,1,0:T(8,128)(2,1)}), bf16[32,48,1024]{2,1,0:T(8,128)(2,1)S(1)}, u32[]{:S(2)}, u32[]{:S(2)}) async-start(bf16[32,48,1024]{2,1,0:T(8,128)(2,1)} %bitcast.49), calls=%async_computation.2 | async-start | bytes 6291456 | tf_op jit(solution)/shard_map/all_to_all | solution.py:313
  80.0 8.4 %copy-start.11 = (f32[1,32]{1,0:T(1,128)S(1)}, f32[1,32]{1,0:T(1,128)}, u32[]{:S(2)}) copy-start(f32[1,32]{1,0:T(1,128)} %param.14) | copy-start | bytes 388
  84.8 182.1 %collective-permute-start.8 = (bf16[1024,2048]{1,0:T(8,128)(2,1)}, bf16[1024,2048]{1,0:T(8,128)(2,1)}, u32[]{:S(2)}, u32[]{:S(2)}) collective-permute-start(bf16[1024,2048]{1,0:T(8,128)(2,1)} %constant_dynamic-slice_fusion), channel_id=1, source_target_pairs={{0,3},{1,0},{2,1},{3,2},{4,7},{5,4},{6,5},{7,6},{8,11},{9,8},{10,9... | collective-permute-start | bytes 12582920 | tf_op jit(solution)/shard_map/ppermute | solution.py:330
  87.3 181.0 %collective-permute-start.7 = (bf16[1024,2048]{1,0:T(8,128)(2,1)}, bf16[1024,2048]{1,0:T(8,128)(2,1)}, u32[]{:S(2)}, u32[]{:S(2)}) collective-permute-start(bf16[1024,2048]{1,0:T(8,128)(2,1)} %constant_dynamic-slice_fusion), channel_id=1, source_target_pairs={{0,2},{1,3},{2,0},{3,1},{4,6},{5,7},{6,4},{7,5},{8,10},{9,11},{10,... | collective-permute-start | bytes 12582920 | tf_op jit(solution)/shard_map/ppermute | solution.py:330
  87.8 183.7 %collective-permute-start.6 = (bf16[1024,2048]{1,0:T(8,128)(2,1)}, bf16[1024,2048]{1,0:T(8,128)(2,1)}, u32[]{:S(2)}, u32[]{:S(2)}) collective-permute-start(bf16[1024,2048]{1,0:T(8,128)(2,1)} %constant_dynamic-slice_fusion), channel_id=1, source_target_pairs={{0,1},{1,2},{2,3},{3,0},{4,5},{5,6},{6,7},{7,4},{8,9},{9,10},{10,1... | collective-permute-start | bytes 12582920 | tf_op jit(solution)/shard_map/ppermute | solution.py:330
  119.9 14.3 %copy-start = (bf16[32,48,1024]{2,1,0:T(8,128)(2,1)}, bf16[32,48,1024]{2,1,0:T(8,128)(2,1)S(1)}, u32[]{:S(2)}) copy-start(bf16[32,48,1024]{2,1,0:T(8,128)(2,1)S(1)} %all-to-all-done.2) | copy-start | bytes 9437188
  119.9 170.6 %all-to-all-start.3 = ((bf16[32,48,1024]{2,1,0:T(8,128)(2,1)}), bf16[32,48,1024]{2,1,0:T(8,128)(2,1)}, u32[]{:S(2)}, u32[]{:S(2)}) async-start(bf16[32,48,1024]{2,1,0:T(8,128)(2,1)} %bitcast.48), calls=%async_computation.3 | async-start | bytes 6291456 | tf_op jit(solution)/shard_map/all_to_all | solution.py:313
  266.9 119.1 %collective-permute-start.11 = (bf16[1024,2048]{1,0:T(8,128)(2,1)}, bf16[1024,2048]{1,0:T(8,128)(2,1)}, u32[]{:S(2)}, u32[]{:S(2)}) collective-permute-start(bf16[1024,2048]{1,0:T(8,128)(2,1)} %collective-permute-done.8.refs_11_), channel_id=1, source_target_pairs={{0,4},{4,0},{8,12},{12,8},{16,20},{20,16},{24,28},{28,24},{32,36},... | collective-permute-start | bytes 12582920 | tf_op jit(solution)/shard_map/ppermute | solution.py:333
  268.3 117.7 %collective-permute-start.10 = (bf16[1024,2048]{1,0:T(8,128)(2,1)}, bf16[1024,2048]{1,0:T(8,128)(2,1)}, u32[]{:S(2)}, u32[]{:S(2)}) collective-permute-start(bf16[1024,2048]{1,0:T(8,128)(2,1)} %collective-permute-done.7.refs_10_), channel_id=1, source_target_pairs={{0,4},{4,0},{8,12},{12,8},{16,20},{20,16},{24,28},{28,24},{32,36},... | collective-permute-start | bytes 12582920 | tf_op jit(solution)/shard_map/ppermute | solution.py:333
  271.5 114.5 %collective-permute-start.9 = (bf16[1024,2048]{1,0:T(8,128)(2,1)}, bf16[1024,2048]{1,0:T(8,128)(2,1)}, u32[]{:S(2)}, u32[]{:S(2)}) collective-permute-start(bf16[1024,2048]{1,0:T(8,128)(2,1)} %collective-permute-done.6.refs_9_), channel_id=1, source_target_pairs={{0,4},{4,0},{8,12},{12,8},{16,20},{20,16},{24,28},{28,24},{32,36},... | collective-permute-start | bytes 12582920 | tf_op jit(solution)/shard_map/ppermute | solution.py:333
  304.2 29.4 %all-to-all-start.4 = ((bf16[32,48,512]{2,1,0:T(8,128)(2,1)}), bf16[32,48,512]{2,1,0:T(8,128)(2,1)S(1)}, u32[]{:S(2)}, u32[]{:S(2)}) async-start(bf16[32,48,512]{2,1,0:T(8,128)(2,1)} %bitcast.54), calls=%async_computation.4 | async-start | bytes 3145728 | tf_op jit(solution)/shard_map/all_to_all | solution.py:313
  333.7 7.3 %copy-start.3 = (bf16[32,48,512]{2,1,0:T(8,128)(2,1)}, bf16[32,48,512]{2,1,0:T(8,128)(2,1)S(1)}, u32[]{:S(2)}) copy-start(bf16[32,48,512]{2,1,0:T(8,128)(2,1)S(1)} %all-to-all-done.4) | copy-start | bytes 4718596
  333.7 27.9 %all-to-all-start.5 = ((bf16[32,48,512]{2,1,0:T(8,128)(2,1)}), bf16[32,48,512]{2,1,0:T(8,128)(2,1)S(1)}, u32[]{:S(2)}, u32[]{:S(2)}) async-start(bf16[32,48,512]{2,1,0:T(8,128)(2,1)} %bitcast.51), calls=%async_computation.5 | async-start | bytes 3145728 | tf_op jit(solution)/shard_map/all_to_all | solution.py:313
  345.1 21.8 %copy-start.12 = (bf16[256,512]{1,0:T(8,128)(2,1)S(1)}, bf16[256,512]{1,0:T(8,128)(2,1)}, u32[]{:S(2)}) copy-start(bf16[256,512]{1,0:T(8,128)(2,1)} %get-tuple-element.21) | copy-start | bytes 786436
  345.1 21.8 %collective-permute-start = (bf16[256,512]{1,0:T(8,128)(2,1)}, bf16[256,512]{1,0:T(8,128)(2,1)S(1)}, u32[]{:S(2)}, u32[]{:S(2)}) collective-permute-start(bf16[256,512]{1,0:T(8,128)(2,1)} %get-tuple-element.17), channel_id=1, source_target_pairs={{0,1},{1,2},{2,3},{3,0},{4,5},{5,6},{6,7},{7,4},{8,9},{9,10},{10,1... | collective-permute-start | bytes 786440 | tf_op jit(solution)/shard_map/ppermute | solution.py:330
  345.1 22.3 %collective-permute-start.2 = (bf16[256,512]{1,0:T(8,128)(2,1)}, bf16[256,512]{1,0:T(8,128)(2,1)S(1)}, u32[]{:S(2)}, u32[]{:S(2)}) collective-permute-start(bf16[256,512]{1,0:T(8,128)(2,1)} %get-tuple-element.19), channel_id=1, source_target_pairs={{0,2},{1,3},{2,0},{3,1},{4,6},{5,7},{6,4},{7,5},{8,10},{9,11},{10,... | collective-permute-start | bytes 786440 | tf_op jit(solution)/shard_map/ppermute | solution.py:330
  361.6 1.1 copy-start.2
  366.9 19.1 %copy-start.4 = (bf16[256,512]{1,0:T(8,128)(2,1)}, bf16[256,512]{1,0:T(8,128)(2,1)S(1)}, u32[]{:S(2)}) copy-start(bf16[256,512]{1,0:T(8,128)(2,1)S(1)} %collective-permute-done.refs_2_) | copy-start | bytes 786436
  366.9 6.0 %collective-permute-start.4 = (bf16[256,512]{1,0:T(8,128)(2,1)S(1)}, bf16[256,512]{1,0:T(8,128)(2,1)S(1)}, u32[]{:S(2)}, u32[]{:S(2)}) collective-permute-start(bf16[256,512]{1,0:T(8,128)(2,1)S(1)} %copy-done.12), channel_id=1, source_target_pairs={{0,3},{1,0},{2,1},{3,2},{4,7},{5,4},{6,5},{7,6},{8,11},{9,8},{10,9... | collective-permute-start | bytes 786440 | tf_op jit(solution)/shard_map/ppermute | solution.py:330
  367.3 18.7 %copy-start.5 = (bf16[256,512]{1,0:T(8,128)(2,1)}, bf16[256,512]{1,0:T(8,128)(2,1)S(1)}, u32[]{:S(2)}) copy-start(bf16[256,512]{1,0:T(8,128)(2,1)S(1)} %collective-permute-done.2.refs_4_) | copy-start | bytes 786436
  367.3 7.1 %collective-permute-start.1 = (bf16[256,512]{1,0:T(8,128)(2,1)}, bf16[256,512]{1,0:T(8,128)(2,1)S(1)}, u32[]{:S(2)}, u32[]{:S(2)}) collective-permute-start(bf16[256,512]{1,0:T(8,128)(2,1)} %get-tuple-element.18), channel_id=1, source_target_pairs={{0,1},{1,2},{2,3},{3,0},{4,5},{5,6},{6,7},{7,4},{8,9},{9,10},{10,1... | collective-permute-start | bytes 786440 | tf_op jit(solution)/shard_map/ppermute | solution.py:330
  372.9 13.1 %copy-start.6 = (bf16[256,512]{1,0:T(8,128)(2,1)}, bf16[256,512]{1,0:T(8,128)(2,1)S(1)}, u32[]{:S(2)}) copy-start(bf16[256,512]{1,0:T(8,128)(2,1)S(1)} %collective-permute-done.4.refs_6_) | copy-start | bytes 786436
  372.9 6.9 %collective-permute-start.3 = (bf16[256,512]{1,0:T(8,128)(2,1)}, bf16[256,512]{1,0:T(8,128)(2,1)S(1)}, u32[]{:S(2)}, u32[]{:S(2)}) collective-permute-start(bf16[256,512]{1,0:T(8,128)(2,1)} %get-tuple-element.20), channel_id=1, source_target_pairs={{0,2},{1,3},{2,0},{3,1},{4,6},{5,7},{6,4},{7,5},{8,10},{9,11},{10,... | collective-permute-start | bytes 786440 | tf_op jit(solution)/shard_map/ppermute | solution.py:330
  374.4 11.6 %copy-start.7 = (bf16[256,512]{1,0:T(8,128)(2,1)}, bf16[256,512]{1,0:T(8,128)(2,1)S(1)}, u32[]{:S(2)}) copy-start(bf16[256,512]{1,0:T(8,128)(2,1)S(1)} %collective-permute-done.1.refs_3_) | copy-start | bytes 786436
  374.4 11.6 %collective-permute-start.5 = (bf16[256,512]{1,0:T(8,128)(2,1)}, bf16[256,512]{1,0:T(8,128)(2,1)S(1)}, u32[]{:S(2)}, u32[]{:S(2)}) collective-permute-start(bf16[256,512]{1,0:T(8,128)(2,1)} %get-tuple-element.22), channel_id=1, source_target_pairs={{0,3},{1,0},{2,1},{3,2},{4,7},{5,4},{6,5},{7,6},{8,11},{9,8},{10,9... | collective-permute-start | bytes 786440 | tf_op jit(solution)/shard_map/ppermute | solution.py:330
  379.8 6.2 %copy-start.8 = (bf16[256,512]{1,0:T(8,128)(2,1)}, bf16[256,512]{1,0:T(8,128)(2,1)S(1)}, u32[]{:S(2)}) copy-start(bf16[256,512]{1,0:T(8,128)(2,1)S(1)} %collective-permute-done.3.refs_5_) | copy-start | bytes 786436
  386.0 0.7 copy-start.9

commit v3 on v2

--- a/solution.py
+++ b/solution.py
@@ -13,6 +13,7 @@
 OUT_COLS = 512
 HALVES = 2
 NEG = -1e30
+LANES = 128
 
 VMEM = pl.BlockSpec(memory_space=pltpu.VMEM)
 BIG = pltpu.CompilerParams(vmem_limit_bytes=60 << 20)
@@ -47,15 +48,44 @@
     )(position.reshape(1, tokens), values)
 
 
+def pack_coded_kernel(position_ref, values_ref, codes_ref, packed_ref):
+    rows, tokens = packed_ref.shape[0], values_ref.shape[0]
+    width = values_ref.shape[1]
+    first = pl.program_id(0) * rows
+    row_of = first + lax.broadcasted_iota(jnp.int32, (rows, tokens), 0)
+    pick = (row_of == position_ref[...]).astype(jnp.bfloat16)
+    for ref, low in ((values_ref, 0), (codes_ref, width)):
+        packed_ref[:, low : low + ref.shape[1]] = jnp.dot(
+            pick, ref[...], preferred_element_type=jnp.float32
+        ).astype(jnp.bfloat16)
+
+
+def pack_coded(position, values, codes, rows):
+    tokens, width = values.shape
+    codes = jnp.broadcast_to(codes.astype(jnp.bfloat16)[:, None], (tokens, LANES))
+    return pl.pallas_call(
+        pack_coded_kernel,
+        grid=(rows // PACK_ROWS,),
+        in_specs=[
+            pl.BlockSpec((1, tokens), lambda i: (0, 0)),
+            pl.BlockSpec((tokens, width), lambda i: (0, 0)),
+            pl.BlockSpec((tokens, LANES), lambda i: (0, 0)),
+        ],
+        out_specs=pl.BlockSpec((PACK_ROWS, width + LANES), lambda i: (i, 0)),
+        out_shape=jax.ShapeDtypeStruct((rows, width + LANES), jnp.bfloat16),
+        cost_estimate=cost(2 * rows * tokens * width, 2 * width * (rows + tokens)),
+    )(position.reshape(1, tokens), values, codes)
+
+
 def order_rows(target_ref, rows_ref, ordered_ref, offset):
-    rows = rows_ref.shape[0]
+    rows, width = rows_ref.shape[0], ordered_ref.shape[1]
 
     def order(step, carry):
         start = step * (2 * TILE)
         place = start + lax.broadcasted_iota(jnp.int32, (2 * TILE, rows), 0)
         pick = (place == target_ref[...]).astype(jnp.bfloat16)
         ordered_ref[pl.ds(start + offset, 2 * TILE), :] = jnp.dot(
-            pick, rows_ref[...], preferred_element_type=jnp.float32
+            pick, rows_ref[:, :width], preferred_element_type=jnp.float32
         ).astype(jnp.bfloat16)
         return carry
 
@@ -63,11 +93,11 @@
 
 
 def keys_kernel(target_ref, cluster_ref, rows_ref, sums_ref, counts_ref, ordered_ref, centroids_ref):
-    rows, width = rows_ref.shape
+    rows, width = rows_ref.shape[0], ordered_ref.shape[1]
     clusters = sums_ref.shape[0]
     belongs = lax.broadcasted_iota(jnp.int32, (clusters, rows), 0) == cluster_ref[...]
     batch_sums = jnp.dot(
-        belongs.astype(jnp.bfloat16), rows_ref[...], preferred_element_type=jnp.float32
+        belongs.astype(jnp.bfloat16), rows_ref[:, :width], preferred_element_type=jnp.float32
     )
     batch_counts = jnp.sum(belongs.astype(jnp.float32), axis=1, keepdims=True)
     centroids_ref[...] = (0.6 * sums_ref[...] + 0.4 * batch_sums) / (
@@ -78,7 +108,7 @@
 
 
 def order_keys(target, cluster, rows, sums, counts):
-    total, width = rows.shape
+    total, width = rows.shape[0], sums.shape[1]
     return pl.pallas_call(
         keys_kernel,
         in_specs=[VMEM] * 5,
@@ -215,66 +245,48 @@
 
 
 def project_kernel(core_ref, *refs):
-    groups = (len(refs) - 1) // (HALVES + 2)
-    row_refs = refs[: groups * HALVES]
-    own_ref = refs[groups * HALVES]
-    weight_refs = refs[groups * HALVES + 1 : -2]
-    out_ref, rows_ref = refs[-2:]
+    row_refs, weight_refs, out_ref, rows_ref = refs[:8], refs[8:13], refs[13], refs[14]
     part = row_refs[0].shape[1]
-    width = part * HALVES
     step = pl.program_id(0)
 
-    @pl.when(step == 0)
-    def _():
-        for index, ref in enumerate(row_refs):
-            rows_ref[:, index * part : (index + 1) * part] = ref[...]
-
-    def product(side):
-        total = jnp.dot(rows_ref[:, :width], own_ref[...], preferred_element_type=jnp.float32)
-        for index, ref in enumerate(weight_refs[side * (groups - 1) : (side + 1) * (groups - 1)]):
-            total += jnp.dot(
-                rows_ref[:, (index + 1) * width : (index + 2) * width],
-                ref[...],
-                preferred_element_type=jnp.float32,
-            )
-        out_ref[...] = total.astype(jnp.bfloat16)
-
-    steps = pl.num_programs(0)
-
-    @pl.when(step < steps // 2)
-    def _():
-        product(0)
-
-    @pl.when(step >= steps // 2)
-    def _():
-        product(1)
-
-
-def project(core, rows, own, near, far):
+    for core, pieces in ((0, (0, 1, 2, 3, 6, 7, 4, 5)), (1, (0, 1, 6, 7, 2, 3, 5, 4))):
+
+        @pl.when((step == 0) & (core_ref[0] == core))
+        def _():
+            for index, piece in enumerate(pieces):
+                rows_ref[:, index * part : (index + 1) * part] = row_refs[piece][...]
+
+    total, low = None, 0
+    for ref in weight_refs:
+        depth = ref.shape[0]
+        term = jnp.dot(
+            rows_ref[:, low : low + depth], ref[...], preferred_element_type=jnp.float32
+        )
+        total, low = term if total is None else total + term, low + depth
+    out_ref[...] = total.astype(jnp.bfloat16)
+
+
+def project(core, rows, weights):
     tokens, part = rows[0].shape
-    width, columns = own.shape
-    groups = len(near) + 1
-    steps = columns // OUT_COLS
-    middle = steps // 2
-    placed = lambda i, core: (0, lax.rem(core[0] * middle + i, steps))
+    columns = weights[0].shape[1]
+    depth = sum(value.shape[0] for value in weights)
     return pl.pallas_call(
         project_kernel,
         grid_spec=pltpu.PrefetchScalarGridSpec(
             num_scalar_prefetch=1,
-            grid=(steps,),
+            grid=(columns // OUT_COLS,),
             in_specs=[pl.BlockSpec((tokens, part), lambda i, core: (0, 0))] * len(rows)
-            + [pl.BlockSpec((width, OUT_COLS), placed)]
-            + [pl.BlockSpec((width, OUT_COLS), lambda i, core: (0, jnp.minimum(i, middle - 1)))]
-            * len(near)
-            + [pl.BlockSpec((width, OUT_COLS), lambda i, core: (0, jnp.maximum(i - middle, 0)))]
-            * len(far),
-            out_specs=pl.BlockSpec((tokens, OUT_COLS), placed),
-            scratch_shapes=[pltpu.VMEM((tokens, groups * width), jnp.bfloat16)],
+            + [
+                pl.BlockSpec((value.shape[0], OUT_COLS), lambda i, core: (0, i))
+                for value in weights
+            ],
+            out_specs=pl.BlockSpec((tokens, OUT_COLS), lambda i, core: (0, i)),
+            scratch_shapes=[pltpu.VMEM((tokens, depth), jnp.bfloat16)],
         ),
         out_shape=jax.ShapeDtypeStruct((tokens, columns), jnp.bfloat16),
         compiler_params=BIG,
-        cost_estimate=cost(2 * tokens * groups * width * columns, 2 * groups * width * columns),
-    )(core, *rows, own, *near, *far)
+        cost_estimate=cost(2 * tokens * depth * columns, 2 * depth * columns),
+    )(core, *rows, *weights)
 
 
 def block_positions(cluster_of, owners, per_owner):
@@ -318,7 +330,6 @@
     owners = lax.axis_size("seq")
     groups = lax.axis_size("head")
     tokens = queries.shape[0]
-    columns = out_weight.shape[1]
     per_owner = centroid_sums.shape[1]
     total = owners * SEGMENT
     cluster_of = cluster_ids[0]
@@ -332,47 +343,55 @@
     def swap(value):
         return lax.ppermute(value, "seq", [(i, i ^ 1) for i in range(owners)])
 
+    def spread(value):
+        pairs = [
+            (seq * groups + i, seq * groups + (i + 1 - 2 * (seq % 2)) % groups)
+            for seq in range(owners)
+            for i in range(groups)
+        ]
+        return lax.ppermute(value, ("seq", "head"), pairs)
+
+    def after(value, *others):
+        return lax.optimization_barrier((value, *others))[0]
+
+    near = spread(out_weight)
     position = block_positions(cluster_of, owners, per_owner)
-    packed_keys = pack(position, keys, total)
+    code_of = cluster_of % per_owner * SLOTS + slot_of + 1
+    packed_keys = pack_coded(position, keys, code_of, total)
     rows_keys = exchange(packed_keys, owners)
-
-    position_later, _ = lax.optimization_barrier((position, packed_keys))
-    half_weight = lax.dynamic_slice_in_dim(out_weight, core * (columns // 2), columns // 2, 1)
-    near = [shift(half_weight, by) for by in range(1, groups)]
-    far = [swap(value) for value in near]
-
-    code_of = cluster_of % per_owner * SLOTS + slot_of + 1
-    codes = (
-        jnp.sum(
-            jnp.where(
-                position_later[None, :] == jnp.arange(total, dtype=jnp.int32)[:, None],
-                code_of[None, :],
-                0,
-            ),
-            axis=1,
-        )
-        - 1
-    )
-    codes = lax.all_to_all(codes.reshape(owners, SEGMENT), "seq", 0, 0, tiled=True)
-    rows_queries = exchange(pack(position_later, queries, total), owners)
-    rows_values = exchange(pack(position_later, values, total), owners)
-
+    position_later = after(position, packed_keys)
+    packed_queries = pack(position_later, queries, total)
+    rows_queries = exchange(after(packed_queries, rows_keys), owners)
+    packed_values = pack(after(position_later, packed_queries), values, total)
+    rows_values = exchange(after(packed_values, rows_queries), owners)
+
+    codes = rows_keys[:, keys.shape[1]].astype(jnp.int32).reshape(owners, SEGMENT) - 1
     target, cluster, first = sorted_targets(codes, per_owner)
-    first = jnp.pad(first, (0, 128 - per_owner)).reshape(1, 128)
+    first = jnp.pad(first, (0, LANES - per_owner)).reshape(1, LANES)
     ordered_keys, centroids = order_keys(
         target, cluster, rows_keys, centroid_sums[0], centroid_counts[0][:, None]
     )
     weights = attention_weights(target, first, ordered_keys, rows_queries)
+
+    near = after(near, rows_queries)
+    far = swap(near)
+    depth = out_weight.shape[0] // 2
+    opposite = [spread(lax.dynamic_slice_in_dim(near, core * depth, depth, 0))]
 
     quarter = jnp.arange(groups, dtype=jnp.int32)
     rolled = position.reshape(groups, tokens // groups)[(group + quarter) % groups].reshape(tokens)
     halves = []
     for half in range(HALVES):
-        returned = exchange(attend_half(half, target, weights, rows_values), owners)
+        attended = attend_half(half, target if half == 0 else after(target, attended), weights, rows_values)
+        if half == 0:
+            opposite.append(swap(after(opposite[0], attended)))
+            returned = exchange(attended, owners)
+        else:
+            returned = exchange(after(attended, returned), owners)
         pieces = unpack(rolled, returned, groups)
         halves.append([pieces[0]] + [shift(pieces[by], by) for by in range(1, groups)])
     rows = [halves[half][by] for by in range(groups) for half in range(HALVES)]
-    mixed = project(core.reshape(1), rows, out_weight, near, far)
+    mixed = project(core.reshape(1), rows, [out_weight, near, far, *opposite])
     return (mixed, centroids[None])
 
 

time: 409 us -> 284 us (0.69)
  waiting for transfers between devices: 221 us -> 104 us
  blocking collectives: 16.4 us -> 0 us
  starting transfers between devices: 39.5 us -> 45.5 us
    ppermute x9 -> x6, waiting for transfers between devices: 143 us -> 11.2 us  [shift(): lax.ppermute(value, 'head', [(i, (i + by) % groups) for i in range(groups)])]
    all_to_all x1 -> x0, blocking collectives: 16.4 us -> none  [shards(): lax.all_to_all(codes.reshape(owners, SEGMENT), 'seq', 0, 0, tiled=True)]
    all_to_all x5, waiting for transfers between devices: 78.2 us -> 92.3 us  [exchange(): lax.all_to_all(rows.reshape(owners, SEGMENT, width), 'seq', 0, 0, tiled=T...]
    pallas_call x0 -> x1, Pallas kernels: none -> 7.31 us  [pack_coded(): pl.pallas_call(pack_coded_kernel, grid=(rows // PACK_ROWS,), in_specs=[pl...]
    pallas_call x3 -> x2, Pallas kernels: 19.5 us -> 12.9 us  [pack(): pl.pallas_call(pack_kernel, grid=(rows // PACK_ROWS,), in_specs=[pl.Block...]
    ppermute x0 -> x2, starting transfers between devices: none -> 4.41 us  [spread(): return lax.ppermute(value, ('seq', 'head'), pairs)]
  transfers between devices with their start and end apart: 17 -> 15, of which waited for: 10 -> 8; matrix products, arithmetic and copies ran while one was open for 4% -> 9% of each run, Pallas kernels for 19% -> 30%
where the time goes in v3:
time: 284 us; the launch traced here: 283 us
  waiting for transfers between devices  104 us (37%)
  Pallas kernels  103 us (36%)
  starting transfers between devices  45.5 us (16%)
  local copies, waits for them, and re-layouts  17.9 us (6%)
  other arithmetic  11.7 us (4%)
    all_to_all x5, waiting for transfers between devices, exchange(): lax.all_to_all(rows.reshape(owners, SEGMENT, width), 'seq', 0, 0, tiled=T...  92.3 us
    all_to_all x5, starting transfers between devices, exchange(): lax.all_to_all(rows.reshape(owners, SEGMENT, width), 'seq', 0, 0, tiled=T...  28.7 us
    pallas_call x2, Pallas kernels, attend_half(): pl.pallas_call(attend_kernel, grid=(1,), in_specs=[pl.BlockSpec((1, total...  27.4 us
    pallas_call x1, Pallas kernels, attention_weights(): pl.pallas_call(weights_kernel, in_specs=[VMEM] * 4, out_specs=VMEM, out_s...  18.5 us
    pallas_call x1, Pallas kernels, project(): pl.pallas_call(project_kernel, grid_spec=pltpu.PrefetchScalarGridSpec(num...  17.9 us
    pallas_call x2, Pallas kernels, pack(): pl.pallas_call(pack_kernel, grid=(rows // PACK_ROWS,), in_specs=[pl.Block...  12.9 us
    ppermute x6, waiting for transfers between devices, shift(): lax.ppermute(value, 'head', [(i, (i + by) % groups) for i in range(groups)])  11.2 us
    pallas_call x1, Pallas kernels, order_keys(): pl.pallas_call(keys_kernel, in_specs=[VMEM] * 5, out_specs=[VMEM] * 2, ou...  10.4 us
  transfers between devices with their start and end apart: 15, of which 8 were waited for; matrix products, arithmetic and copies ran while one was open for 9% of the time, Pallas kernels for 30%

profile of v3, /device:TPU:1, one launch (start us, length us, event | category | flops | bytes accessed | tf_op | source)
XLA Modules:
  0.0 282.6 jit_solution(15555555567428620640)
XLA Ops:
  0.6 3.4 %collective-permute-start.6 = (bf16[1024,4096]{1,0:T(8,128)(2,1)}, bf16[1024,4096]{1,0:T(8,128)(2,1)}, u32[]{:S(2)}, u32[]{:S(2)}) collective-permute-start(bf16[1024,4096]{1,0:T(8,128)(2,1)} %refs_8_.1), channel_id=1, source_target_pairs={{0,1},{1,2},{2,3},{3,0},{4,7},{5,4},{6,5},{7,6},{8,9},{9,10},{10,1... | collective-permute-start | bytes 25165832 | tf_op jit(solution)/shard_map/ppermute | solution.py:352
  4.5 2.0 fusion.35
  10.3 7.3 %shard_map.95 = bf16[1536,1152]{1,0:T(8,128)(2,1)} custom-call(s32[1,1024]{1,0:T(1,128)} %multiply_add_fusion.position_ref, bf16[1024,1024]{1,0:T(8,128)(2,1)} %values_ref.3, bf16[1024,128]{1,0:T(8,128)(2,1)} %broadcast_in_dim.35.codes_ref), custom_call_target="tpu_custom_call" | custom-call | flops 3221225472 | bytes 5242880 | tf_op jit(solution)/shard_map/pallas_call | solution.py:66
  17.6 8.2 %all-to-all-start = ((bf16[32,48,1152]{2,1,0:T(8,128)(2,1)}), bf16[32,48,1152]{2,1,0:T(8,128)(2,1)S(1)}, u32[]{:S(2)}, u32[]{:S(2)}) async-start(bf16[32,48,1152]{2,1,0:T(8,128)(2,1)} %bitcast.32), calls=%async_computation | async-start | bytes 7077888 | tf_op jit(solution)/shard_map/all_to_all | solution.py:325
  25.8 6.5 %shard_map.97 = bf16[1536,1024]{1,0:T(8,128)(2,1)} custom-call(s32[1,1024]{1,0:T(1,128)} %bitcast.49, bf16[1024,1024]{1,0:T(8,128)(2,1)} %values_ref.4), custom_call_target="tpu_custom_call" | custom-call | flops 3221225472 | bytes 5242880 | tf_op jit(solution)/shard_map/pallas_call | solution.py:38
  32.3 37.5 %all-to-all-done = bf16[32,48,1152]{2,1,0:T(8,128)(2,1)S(1)} async-done(((bf16[32,48,1152]{2,1,0:T(8,128)(2,1)}), bf16[32,48,1152]{2,1,0:T(8,128)(2,1)S(1)}, u32[]{:S(2)}, u32[]{:S(2)}) %all-to-all-start) | async-done | bytes 3538976 | tf_op jit(solution)/shard_map/all_to_all | solution.py:325
  69.7 7.2 %all-to-all-start.1 = ((bf16[32,48,1024]{2,1,0:T(8,128)(2,1)}), bf16[32,48,1024]{2,1,0:T(8,128)(2,1)}, u32[]{:S(2)}, u32[]{:S(2)}) async-start(bf16[32,48,1024]{2,1,0:T(8,128)(2,1)} %bitcast.36), calls=%async_computation.1 | async-start | bytes 6291456 | tf_op jit(solution)/shard_map/all_to_all | solution.py:325
  78.2 6.4 %shard_map.99 = bf16[1536,1024]{1,0:T(8,128)(2,1)} custom-call(s32[1,1024]{1,0:T(1,128)} %bitcast.50, bf16[1024,1024]{1,0:T(8,128)(2,1)} %values_ref.5), custom_call_target="tpu_custom_call" | custom-call | flops 3221225472 | bytes 5242880 | tf_op jit(solution)/shard_map/pallas_call | solution.py:38
  84.6 32.2 %all-to-all-done.1 = bf16[32,48,1024]{2,1,0:T(8,128)(2,1)} async-done(((bf16[32,48,1024]{2,1,0:T(8,128)(2,1)}), bf16[32,48,1024]{2,1,0:T(8,128)(2,1)}, u32[]{:S(2)}, u32[]{:S(2)}) %all-to-all-start.1) | async-done | bytes 3145760 | tf_op jit(solution)/shard_map/all_to_all | solution.py:325
  116.8 2.5 collective-permute-start.7
  119.3 4.7 %constant_dynamic-slice_fusion = bf16[512,4096]{1,0:T(8,128)(2,1)} fusion(bf16[1024,4096]{1,0:T(8,128)(2,1)} %collective-permute-done.6.refs_9_, s32[]{:T(128)S(6)} %select_n.150), kind=kLoop, calls=%fused_computation.78 | loop fusion | bytes 8388612 | tf_op jit(solution)/shard_map/dynamic_slice | solution.py:379
  128.6 4.0 %all-to-all-start.2 = ((bf16[32,48,1024]{2,1,0:T(8,128)(2,1)}), bf16[32,48,1024]{2,1,0:T(8,128)(2,1)S(1)}, u32[]{:S(2)}, u32[]{:S(2)}) async-start(bf16[32,48,1024]{2,1,0:T(8,128)(2,1)} %bitcast.33), calls=%async_computation.2 | async-start | bytes 6291456 | tf_op jit(solution)/shard_map/all_to_all | solution.py:325
  137.2 10.4 %shard_map.96 = (bf16[1664,1024]{1,0:T(8,128)(2,1)}, f32[32,1024]{1,0:T(8,128)}) custom-call(s32[1,1536]{1,0:T(1,128)} %get-tuple-element.45.target_ref.row_target_ref, s32[1,1536]{1,0:T(1,128)} %get-tuple-element.44.cluster_ref, bf16[1536,1152]{1,0:T(8,128)(2,1)} %bitcast.30, f32[32,1024]{1,0:T(8,128)} %bitcast.52, f32[32,1]{1,0:T(8,128)} %copy.17.counts_ref), custom_call_target="tpu_custom_call" | custom-call | flops 4831838208 | bytes 6291456 | tf_op jit(solution)/shard_map/pallas_call | solution.py:112
  147.6 2.7 fusion.4.column_target_ref
  150.3 18.5 %shard_map.98.weights_ref = bf16[8,1536,256]{2,1,0:T(8,128)(2,1)} custom-call(s32[1,1536]{1,0:T(1,128)} %get-tuple-element.45.target_ref.row_target_ref, s32[1,128]{1,0:T(1,128)} %pad_bitcast_fusion.first_ref, bf16[1664,1024]{1,0:T(8,128)(2,1)} %get-tuple-element.20.keys_ref, bf16[1536,1024]{1,0:T(8,128)(2,1)} %bitcast.13.rows_ref), custom_call_target="tpu_custom_call" | custom-call | flops 9663676416 | bytes 12582912 | tf_op jit(solution)/shard_map/pallas_call | solution.py:156
  168.8 3.1 %all-to-all-done.2 = bf16[32,48,1024]{2,1,0:T(8,128)(2,1)S(1)} async-done(((bf16[32,48,1024]{2,1,0:T(8,128)(2,1)}), bf16[32,48,1024]{2,1,0:T(8,128)(2,1)S(1)}, u32[]{:S(2)}, u32[]{:S(2)}) %all-to-all-start.2) | async-done | bytes 3145760 | tf_op jit(solution)/shard_map/all_to_all | solution.py:325
  171.9 1.6 copy-done.1
  173.6 13.7 %shard_map.100 = bf16[1536,512]{1,0:T(8,128)(2,1)} custom-call(s32[1,1536]{1,0:T(1,128)} %get-tuple-element.45.target_ref.row_target_ref, s32[1536,1]{1,0:T(8,128)} %fusion.4.column_target_ref, bf16[8,1536,256]{2,1,0:T(8,128)(2,1)} %shard_map.98.weights_ref, bf16[1536,1024]{1,0:T(8,128)(2,1)} %bitcast.34), custom_call_target="tpu_custom_call" | custom-call | flops 4831838208 | bytes 6291456 | tf_op jit(solution)/shard_map/pallas_call | solution.py:203
  187.2 2.8 %collective-permute-start.9 = (bf16[512,4096]{1,0:T(8,128)(2,1)}, bf16[512,4096]{1,0:T(8,128)(2,1)}, u32[]{:S(2)}, u32[]{:S(2)}) collective-permute-start(bf16[512,4096]{1,0:T(8,128)(2,1)} %collective-permute-done.8.refs_11_), channel_id=1, source_target_pairs={{0,4},{4,0},{8,12},{12,8},{16,20},{20,16},{24,28},{28,24},{32,36},... | collective-permute-start | bytes 12582920 | tf_op jit(solution)/shard_map/ppermute | solution.py:344
  190.1 3.8 %all-to-all-start.3 = ((bf16[32,48,512]{2,1,0:T(8,128)(2,1)}), bf16[32,48,512]{2,1,0:T(8,128)(2,1)S(1)}, u32[]{:S(2)}, u32[]{:S(2)}) async-start(bf16[32,48,512]{2,1,0:T(8,128)(2,1)} %bitcast.40), calls=%async_computation.3 | async-start | bytes 3145728 | tf_op jit(solution)/shard_map/all_to_all | solution.py:325
  195.8 13.7 %shard_map.102 = bf16[1536,512]{1,0:T(8,128)(2,1)} custom-call(s32[1,1536]{1,0:T(1,128)} %reshape.303.row_target_ref, s32[1536,1]{1,0:T(8,128)} %reshape.315.column_target_ref, bf16[8,1536,256]{2,1,0:T(8,128)(2,1)} %shard_map.98.weights_ref, bf16[1536,1024]{1,0:T(8,128)(2,1)} %bitcast.35), custom_call_target="tpu_custom_call" | custom-call | flops 4831838208 | bytes 6291456 | tf_op jit(solution)/shard_map/pallas_call | solution.py:203
  209.6 6.5 %all-to-all-done.3 = bf16[32,48,512]{2,1,0:T(8,128)(2,1)S(1)} async-done(((bf16[32,48,512]{2,1,0:T(8,128)(2,1)}), bf16[32,48,512]{2,1,0:T(8,128)(2,1)S(1)}, u32[]{:S(2)}, u32[]{:S(2)}) %all-to-all-start.3) | async-done | bytes 1572896 | tf_op jit(solution)/shard_map/all_to_all | solution.py:325
  216.1 5.5 %all-to-all-start.4 = ((bf16[32,48,512]{2,1,0:T(8,128)(2,1)}), bf16[32,48,512]{2,1,0:T(8,128)(2,1)S(1)}, u32[]{:S(2)}, u32[]{:S(2)}) async-start(bf16[32,48,512]{2,1,0:T(8,128)(2,1)} %bitcast.37), calls=%async_computation.4 | async-start | bytes 3145728 | tf_op jit(solution)/shard_map/all_to_all | solution.py:325
  223.3 4.1 %shard_map.101 = (bf16[256,512]{1,0:T(8,128)(2,1)}, bf16[256,512]{1,0:T(8,128)(2,1)}, bf16[256,512]{1,0:T(8,128)(2,1)}, bf16[256,512]{1,0:T(8,128)(2,1)}) custom-call(s32[1024,1]{1,0:T(8,128)} %bitcast.41, bf16[1536,512]{1,0:T(8,128)(2,1)} %bitcast.39), custom_call_target="tpu_custom_call" | custom-call | flops 1610612736 | bytes 2621440 | tf_op jit(solution)/shard_map/pallas_call | solution.py:238
  228.4 2.2 collective-permute-start.2
  231.0 13.0 %all-to-all-done.4 = bf16[32,48,512]{2,1,0:T(8,128)(2,1)S(1)} async-done(((bf16[32,48,512]{2,1,0:T(8,128)(2,1)}), bf16[32,48,512]{2,1,0:T(8,128)(2,1)S(1)}, u32[]{:S(2)}, u32[]{:S(2)}) %all-to-all-start.4) | async-done | bytes 1572896 | tf_op jit(solution)/shard_map/all_to_all | solution.py:325
  245.1 4.1 %shard_map.103 = (bf16[256,512]{1,0:T(8,128)(2,1)}, bf16[256,512]{1,0:T(8,128)(2,1)}, bf16[256,512]{1,0:T(8,128)(2,1)}, bf16[256,512]{1,0:T(8,128)(2,1)}) custom-call(s32[1024,1]{1,0:T(8,128)} %bitcast.42, bf16[1536,512]{1,0:T(8,128)(2,1)} %bitcast.38), custom_call_target="tpu_custom_call" | custom-call | flops 1610612736 | bytes 2621440 | tf_op jit(solution)/shard_map/pallas_call | solution.py:238
  250.2 2.2 collective-permute-start.3
  252.8 3.8 %collective-permute-done.1.refs_3_ = bf16[256,512]{1,0:T(8,128)(2,1)S(1)} collective-permute-done((bf16[256,512]{1,0:T(8,128)(2,1)}, bf16[256,512]{1,0:T(8,128)(2,1)S(1)}, u32[]{:S(2)}, u32[]{:S(2)}) %collective-permute-start.1) | collective-permute-done | bytes 262176 | tf_op jit(solution)/shard_map/ppermute | solution.py:341
  256.6 6.0 %collective-permute-done.3.refs_5_ = bf16[256,512]{1,0:T(8,128)(2,1)S(1)} collective-permute-done((bf16[256,512]{1,0:T(8,128)(2,1)}, bf16[256,512]{1,0:T(8,128)(2,1)S(1)}, u32[]{:S(2)}, u32[]{:S(2)}) %collective-permute-start.3) | collective-permute-done | bytes 262176 | tf_op jit(solution)/shard_map/ppermute | solution.py:341
  262.6 1.4 collective-permute-done.5.refs_7_
  264.7 17.9 %shard_map.104 = bf16[256,4096]{1,0:T(8,128)(2,1)} custom-call(s32[1]{0:T(128)} %bitcast.core_ref, bf16[256,512]{1,0:T(8,128)(2,1)} %get-tuple-element.25.refs_0_, bf16[256,512]{1,0:T(8,128)(2,1)} %get-tuple-element.28.refs_1_, bf16[256,512]{1,0:T(8,128)(2,1)} %copy-done.4, bf16[256,512]{1,0:T(8,128)(2,1)} %copy-done.7, bf16[256,512]{1,0:T(8,128)(2,1)} %copy-done.5, ...), custom_call_target="tpu_custom_call" | custom-call | flops 8589934592 | bytes 33554432 | tf_op jit(solution)/shard_map/pallas_call | solution.py:273
  (84 shorter events, 22.8 us)
Async XLA Ops:
  0.6 116.2 %collective-permute-start.6 = (bf16[1024,4096]{1,0:T(8,128)(2,1)}, bf16[1024,4096]{1,0:T(8,128)(2,1)}, u32[]{:S(2)}, u32[]{:S(2)}) collective-permute-start(bf16[1024,4096]{1,0:T(8,128)(2,1)} %refs_8_.1), channel_id=1, source_target_pairs={{0,1},{1,2},{2,3},{3,0},{4,7},{5,4},{6,5},{7,6},{8,9},{9,10},{10,1... | collective-permute-start | bytes 25165832 | tf_op jit(solution)/shard_map/ppermute | solution.py:352
  17.6 52.2 %all-to-all-start = ((bf16[32,48,1152]{2,1,0:T(8,128)(2,1)}), bf16[32,48,1152]{2,1,0:T(8,128)(2,1)S(1)}, u32[]{:S(2)}, u32[]{:S(2)}) async-start(bf16[32,48,1152]{2,1,0:T(8,128)(2,1)} %bitcast.32), calls=%async_computation | async-start | bytes 7077888 | tf_op jit(solution)/shard_map/all_to_all | solution.py:325
  32.3 44.6 %copy-start.18 = (f32[1,32]{1,0:T(1,128)S(1)}, f32[1,32]{1,0:T(1,128)}, u32[]{:S(2)}) copy-start(f32[1,32]{1,0:T(1,128)} %param.14) | copy-start | bytes 388
  69.7 57.3 %copy-start = (bf16[32,48,1152]{2,1,0:T(8,128)(2,1)}, bf16[32,48,1152]{2,1,0:T(8,128)(2,1)S(1)}, u32[]{:S(2)}) copy-start(bf16[32,48,1152]{2,1,0:T(8,128)(2,1)S(1)} %all-to-all-done) | copy-start | bytes 10616836
  69.7 47.1 %all-to-all-start.1 = ((bf16[32,48,1024]{2,1,0:T(8,128)(2,1)}), bf16[32,48,1024]{2,1,0:T(8,128)(2,1)}, u32[]{:S(2)}, u32[]{:S(2)}) async-start(bf16[32,48,1024]{2,1,0:T(8,128)(2,1)} %bitcast.36), calls=%async_computation.1 | async-start | bytes 6291456 | tf_op jit(solution)/shard_map/all_to_all | solution.py:325
  116.8 147.2 %collective-permute-start.7 = (bf16[1024,4096]{1,0:T(8,128)(2,1)}, bf16[1024,4096]{1,0:T(8,128)(2,1)}, u32[]{:S(2)}, u32[]{:S(2)}) collective-permute-start(bf16[1024,4096]{1,0:T(8,128)(2,1)} %collective-permute-done.6.refs_9_), channel_id=1, source_target_pairs={{0,4},{4,0},{8,12},{12,8},{16,20},{20,16},{24,28},{28,24},{32,36},... | collective-permute-start | bytes 25165832 | tf_op jit(solution)/shard_map/ppermute | solution.py:344
  124.1 63.2 %collective-permute-start.8 = (bf16[512,4096]{1,0:T(8,128)(2,1)}, bf16[512,4096]{1,0:T(8,128)(2,1)}, u32[]{:S(2)}, u32[]{:S(2)}) collective-permute-start(bf16[512,4096]{1,0:T(8,128)(2,1)} %constant_dynamic-slice_fusion), channel_id=1, source_target_pairs={{0,1},{1,2},{2,3},{3,0},{4,7},{5,4},{6,5},{7,6},{8,9},{9,10},{10,1... | collective-permute-start | bytes 12582920 | tf_op jit(solution)/shard_map/ppermute | solution.py:352
  125.7 0.7 copy-start.13
  128.6 7.9 %copy-start.14 = (pred[1536]{0:T(1024)(128)(4,1)S(1)}, pred[1536]{0:T(1024)(128)(4,1)}, u32[]{:S(2)}) copy-start(pred[1536]{0:T(1024)(128)(4,1)} %copy-done.13) | copy-start | bytes 4612
  128.6 7.9 %copy-start.16 = (pred[1536]{0:T(1024)(128)(4,1)S(1)}, pred[1536]{0:T(1024)(128)(4,1)}, u32[]{:S(2)}) copy-start(pred[1536]{0:T(1024)(128)(4,1)} %copy-done.15) | copy-start | bytes 4612
  128.6 43.3 %all-to-all-start.2 = ((bf16[32,48,1024]{2,1,0:T(8,128)(2,1)}), bf16[32,48,1024]{2,1,0:T(8,128)(2,1)S(1)}, u32[]{:S(2)}, u32[]{:S(2)}) async-start(bf16[32,48,1024]{2,1,0:T(8,128)(2,1)} %bitcast.33), calls=%async_computation.2 | async-start | bytes 6291456 | tf_op jit(solution)/shard_map/all_to_all | solution.py:325
  171.9 1.6 copy-start.1
  173.5 20.3 %copy-start.10 = (pred[32,48]{1,0:T(8,128)(4,1)S(1)}, pred[32,48]{1,0:T(8,128)(4,1)}, u32[]{:S(2)}) copy-start(pred[32,48]{1,0:T(8,128)(4,1)} %lt.119) | copy-start | bytes 4612
  187.2 76.8 %collective-permute-start.9 = (bf16[512,4096]{1,0:T(8,128)(2,1)}, bf16[512,4096]{1,0:T(8,128)(2,1)}, u32[]{:S(2)}, u32[]{:S(2)}) collective-permute-start(bf16[512,4096]{1,0:T(8,128)(2,1)} %collective-permute-done.8.refs_11_), channel_id=1, source_target_pairs={{0,4},{4,0},{8,12},{12,8},{16,20},{20,16},{24,28},{28,24},{32,36},... | collective-permute-start | bytes 12582920 | tf_op jit(solution)/shard_map/ppermute | solution.py:344
  190.1 26.0 %all-to-all-start.3 = ((bf16[32,48,512]{2,1,0:T(8,128)(2,1)}), bf16[32,48,512]{2,1,0:T(8,128)(2,1)S(1)}, u32[]{:S(2)}, u32[]{:S(2)}) async-start(bf16[32,48,512]{2,1,0:T(8,128)(2,1)} %bitcast.40), calls=%async_computation.3 | async-start | bytes 3145728 | tf_op jit(solution)/shard_map/all_to_all | solution.py:325
  195.8 25.8 %copy-start.12 = (s32[1024]{0:T(1024)S(1)}, s32[1024]{0:T(1024)}, u32[]{:S(2)}) copy-start(s32[1024]{0:T(1024)} %copy-done.11) | copy-start | bytes 12292
  195.8 25.8 %copy-start.17 = (s32[1024]{0:T(1024)S(1)}, s32[1024]{0:T(1024)}, u32[]{:S(2)}) copy-start(s32[1024]{0:T(1024)} %get-tuple-element.48) | copy-start | bytes 12292
  216.1 7.3 %copy-start.3 = (bf16[32,48,512]{2,1,0:T(8,128)(2,1)}, bf16[32,48,512]{2,1,0:T(8,128)(2,1)S(1)}, u32[]{:S(2)}) copy-start(bf16[32,48,512]{2,1,0:T(8,128)(2,1)S(1)} %all-to-all-done.3) | copy-start | bytes 4718596
  216.1 27.9 %all-to-all-start.4 = ((bf16[32,48,512]{2,1,0:T(8,128)(2,1)}), bf16[32,48,512]{2,1,0:T(8,128)(2,1)S(1)}, u32[]{:S(2)}, u32[]{:S(2)}) async-start(bf16[32,48,512]{2,1,0:T(8,128)(2,1)} %bitcast.37), calls=%async_computation.4 | async-start | bytes 3145728 | tf_op jit(solution)/shard_map/all_to_all | solution.py:325
  227.4 21.8 %collective-permute-start = (bf16[256,512]{1,0:T(8,128)(2,1)}, bf16[256,512]{1,0:T(8,128)(2,1)S(1)}, u32[]{:S(2)}, u32[]{:S(2)}) collective-permute-start(bf16[256,512]{1,0:T(8,128)(2,1)} %get-tuple-element.29), channel_id=1, source_target_pairs={{0,1},{1,2},{2,3},{3,0},{4,5},{5,6},{6,7},{7,4},{8,9},{9,10},{10,1... | collective-permute-start | bytes 786440 | tf_op jit(solution)/shard_map/ppermute | solution.py:341
  228.4 21.8 %collective-permute-start.2 = (bf16[256,512]{1,0:T(8,128)(2,1)}, bf16[256,512]{1,0:T(8,128)(2,1)S(1)}, u32[]{:S(2)}, u32[]{:S(2)}) collective-permute-start(bf16[256,512]{1,0:T(8,128)(2,1)} %get-tuple-element.31), channel_id=1, source_target_pairs={{0,2},{1,3},{2,0},{3,1},{4,6},{5,7},{6,4},{7,5},{8,10},{9,11},{10,... | collective-permute-start | bytes 786440 | tf_op jit(solution)/shard_map/ppermute | solution.py:341
  230.5 21.8 %collective-permute-start.4 = (bf16[256,512]{1,0:T(8,128)(2,1)}, bf16[256,512]{1,0:T(8,128)(2,1)S(1)}, u32[]{:S(2)}, u32[]{:S(2)}) collective-permute-start(bf16[256,512]{1,0:T(8,128)(2,1)} %get-tuple-element.33), channel_id=1, source_target_pairs={{0,3},{1,0},{2,1},{3,2},{4,7},{5,4},{6,5},{7,6},{8,11},{9,8},{10,9... | collective-permute-start | bytes 786440 | tf_op jit(solution)/shard_map/ppermute | solution.py:341
  244.0 1.1 copy-start.2
  249.2 14.8 %copy-start.4 = (bf16[256,512]{1,0:T(8,128)(2,1)}, bf16[256,512]{1,0:T(8,128)(2,1)S(1)}, u32[]{:S(2)}) copy-start(bf16[256,512]{1,0:T(8,128)(2,1)S(1)} %collective-permute-done.refs_2_) | copy-start | bytes 786436
  249.2 7.4 %collective-permute-start.1 = (bf16[256,512]{1,0:T(8,128)(2,1)}, bf16[256,512]{1,0:T(8,128)(2,1)S(1)}, u32[]{:S(2)}, u32[]{:S(2)}) collective-permute-start(bf16[256,512]{1,0:T(8,128)(2,1)} %get-tuple-element.30), channel_id=1, source_target_pairs={{0,1},{1,2},{2,3},{3,0},{4,5},{5,6},{6,7},{7,4},{8,9},{9,10},{10,1... | collective-permute-start | bytes 786440 | tf_op jit(solution)/shard_map/ppermute | solution.py:341
  250.2 13.9 %copy-start.5 = (bf16[256,512]{1,0:T(8,128)(2,1)}, bf16[256,512]{1,0:T(8,128)(2,1)S(1)}, u32[]{:S(2)}) copy-start(bf16[256,512]{1,0:T(8,128)(2,1)S(1)} %collective-permute-done.2.refs_4_) | copy-start | bytes 786436
  250.2 12.5 %collective-permute-start.3 = (bf16[256,512]{1,0:T(8,128)(2,1)}, bf16[256,512]{1,0:T(8,128)(2,1)S(1)}, u32[]{:S(2)}, u32[]{:S(2)}) collective-permute-start(bf16[256,512]{1,0:T(8,128)(2,1)} %get-tuple-element.32), channel_id=1, source_target_pairs={{0,2},{1,3},{2,0},{3,1},{4,6},{5,7},{6,4},{7,5},{8,10},{9,11},{10,... | collective-permute-start | bytes 786440 | tf_op jit(solution)/shard_map/ppermute | solution.py:341
  252.3 11.7 %copy-start.6 = (bf16[256,512]{1,0:T(8,128)(2,1)}, bf16[256,512]{1,0:T(8,128)(2,1)S(1)}, u32[]{:S(2)}) copy-start(bf16[256,512]{1,0:T(8,128)(2,1)S(1)} %collective-permute-done.4.refs_6_) | copy-start | bytes 786436
  252.3 11.7 %collective-permute-start.5 = (bf16[256,512]{1,0:T(8,128)(2,1)}, bf16[256,512]{1,0:T(8,128)(2,1)S(1)}, u32[]{:S(2)}, u32[]{:S(2)}) collective-permute-start(bf16[256,512]{1,0:T(8,128)(2,1)} %get-tuple-element.34), channel_id=1, source_target_pairs={{0,3},{1,0},{2,1},{3,2},{4,7},{5,4},{6,5},{7,6},{8,11},{9,8},{10,9... | collective-permute-start | bytes 786440 | tf_op jit(solution)/shard_map/ppermute | solution.py:341
  256.6 7.4 %copy-start.7 = (bf16[256,512]{1,0:T(8,128)(2,1)}, bf16[256,512]{1,0:T(8,128)(2,1)S(1)}, u32[]{:S(2)}) copy-start(bf16[256,512]{1,0:T(8,128)(2,1)S(1)} %collective-permute-done.1.refs_3_) | copy-start | bytes 786436
  262.6 1.4 copy-start.8
  264.0 0.7 copy-start.9
  (2 other events, 1.3 us)
